TPU v7x, 256 devices: a whole 4x4x8 slice. The times are simulated.
256 devices in a mesh: lat: 16 (over z, x_hi), lon: 16 (over x_lo, y, core).
Axes of the slice: x: 4 (x_hi: 2, x_lo: 2; x = x_hi * 2 + x_lo), y: 4, z: 8, core: 2. Of those that a mesh axis runs over, the one named last changes fastest.
Arguments:
- displacement: float32 [32, 384, 2048], P(None, 'lat', 'lon'), may hold values from -6 to 6
- materials: int32 [32, 384, 2048], P(None, 'lat', 'lon'), may hold values from 0 to 3
- ice_mask: int32 [384, 2048], P('lat', 'lon'), may hold values 0 or 1
- ice_height: float32 [384, 2048], P('lat', 'lon'), may hold values from 0.5 to 3
- shear: float32 [4], replicated, may hold values from 0.5 to 4
- restoring: float32 [4], replicated, may hold values from 0.5 to 2
- contrast: float32 [4], replicated, may hold values from 0.3 to 3
- green: float32 [256, 32, 32], P('lat'), may hold values from -1 to 1
Outputs:
- final_displacement: float32 [32, 384, 2048], P(None, 'lat', 'lon')
- potential: float32 [32, 384, 2048], P(None, 'lat', 'lon')
All inputs are finite; a program needn't handle non-finite values. No bound on the sum of `ice_mask` on one device may be relied on, other than what follows from the above.
Results may differ from a plain program's by a relative error of at most 0.0003.
Values sent between devices are 32-bit elements; how exact they have to be, the bound alone decides.
A program may use at most 128 MiB of HBM per device.

v0:
```python
import jax
import jax.numpy as jnp
from jax import lax
from jax.sharding import PartitionSpec as P

LMAX = 256
NMAT = 4
ITERS = 2
SWEEPS = 4


def extended(cells, sides, width, closed):
    for axis, dim in sides:
        count = lax.axis_size(axis)
        ends = count if closed else count - 1
        head = lax.slice_in_dim(cells, 0, width, axis=dim)
        tail = lax.slice_in_dim(cells, cells.shape[dim] - width, cells.shape[dim], axis=dim)
        cells = jnp.concatenate(
            [
                lax.ppermute(tail, axis, [(i, (i + 1) % count) for i in range(ends)]),
                cells,
                lax.ppermute(head, axis, [((i + 1) % count, i) for i in range(ends)]),
            ],
            axis=dim,
        )
    return cells


def split_up(array, dim, devices):
    before, after = (array.shape[:dim], array.shape[dim + 1 :])
    return jnp.moveaxis(array.reshape(*before, devices, -1, *after), dim, 0)


def sum_at_owner(array, axis, dim):
    devices = lax.axis_size(axis)
    pieces = lax.all_to_all(split_up(array, dim, devices), axis, 0, 0, tiled=True)
    return jnp.sum(pieces, axis=0)


def from_everyone(array, axis):
    copies = jnp.broadcast_to(array, (lax.axis_size(axis), *array.shape))
    return lax.all_to_all(copies, axis, split_axis=0, concat_axis=0, tiled=True)


def laid_out(pieces, dim):
    pieces = jnp.moveaxis(pieces, 0, dim)
    shape = pieces.shape
    return pieces.reshape(*shape[:dim], shape[dim] * shape[dim + 1], *shape[dim + 2 :])


def collect(array, axis, dim):
    pieces = from_everyone(array, axis)
    return laid_out(pieces, dim)


def legendre(theta):
    orders = jnp.arange(LMAX)
    order_f = orders.astype(jnp.float32)
    cosine = jnp.cos(theta)[:, None]
    sine = jnp.sin(theta)[:, None]
    safe = jnp.maximum(order_f, 1.0)
    growth = jnp.where(orders >= 2, 0.5 * jnp.log((2.0 * safe + 1.0) / (2.0 * safe)), 0.0)
    log_diag = jnp.where(orders >= 1, 0.5 * jnp.log(3.0) + jnp.cumsum(growth), 0.0)
    diagonal = jnp.exp(log_diag[None, :] + order_f[None, :] * jnp.log(sine))

    def advance(carry, degree):
        prev_one, prev_two = carry
        deg_f = degree.astype(jnp.float32)
        first = jnp.sqrt(
            (4.0 * deg_f * deg_f - 1.0) / jnp.maximum(deg_f * deg_f - order_f * order_f, 1.0)
        )
        second = jnp.sqrt(
            jnp.maximum((deg_f - 1.0) ** 2 - order_f * order_f, 0.0)
            / jnp.maximum(4.0 * (deg_f - 1.0) ** 2 - 1.0, 1.0)
        )
        general = first * (cosine * prev_one - second * prev_two)
        start_next = jnp.sqrt(2.0 * order_f + 3.0) * cosine * diagonal
        value = jnp.where(
            orders == degree,
            diagonal,
            jnp.where(
                orders == degree - 1, start_next, jnp.where(orders < degree - 1, general, 0.0)
            ),
        )
        return ((value, prev_one), value)

    zeros = jnp.zeros((theta.shape[0], LMAX), jnp.float32)
    _, table = lax.scan(advance, (zeros, zeros), jnp.arange(LMAX), unroll=8)
    return table


def fourier_tables(columns, total):
    orders = jnp.arange(LMAX)
    phase = columns[:, None] * orders[None, :] % total
    angle = 2.0 * jnp.pi / total * phase.astype(jnp.float32)
    forward = jnp.concatenate([jnp.cos(angle), jnp.sin(angle)], axis=1) * (2.0 * jnp.pi / total)
    inverse = jnp.concatenate([jnp.cos(angle), jnp.sin(angle)], axis=1).T
    return (forward, inverse)


def lookup(materials, table):
    result = jnp.zeros(materials.shape, jnp.float32)
    for material in range(NMAT):
        result = result + jnp.where(materials == material, table[material], 0.0)
    return result


def crop_block(block, margin):
    return block[:, margin : block.shape[1] - margin, margin : block.shape[2] - margin]


def margin_sweeps(field, force, stiff, restore, depth, lat_first, total_lat):
    stacked = jnp.stack([field, force, stiff, restore], axis=0)
    lat_wide = extended(stacked, (("lat", 2),), depth, False)
    wide = extended(lat_wide, (("lon", 3),), depth, True)
    current = wide[0]
    rows_wide = wide.shape[2]
    global_rows = lat_first - depth + jnp.arange(rows_wide)
    inside = ((global_rows >= 0) & (global_rows < total_lat))[None, :, None]
    for step in range(depth):
        margin = step + 1
        inner = current[:, 1:-1, 1:-1]
        beside_all = (
            current[:, 2:, 1:-1]
            + current[:, :-2, 1:-1]
            + current[:, 1:-1, 2:]
            + current[:, 1:-1, :-2]
        )
        layer_pad = jnp.pad(inner, ((1, 1), (0, 0), (0, 0)))
        beside_all = beside_all + layer_pad[2:] + layer_pad[:-2]
        force_part = crop_block(wide[1], margin)
        stiff_part = crop_block(wide[2], margin)
        restore_part = crop_block(wide[3], margin)
        valid = inside[:, margin : rows_wide - margin, :]
        denominator = jnp.where(valid, 6.0 * stiff_part + restore_part, 1.0)
        current = jnp.where(valid, (force_part + stiff_part * beside_all) / denominator, 0.0)
    return current


def on_device(displacement, materials, ice_mask, ice_height, shear, restoring, contrast, green):
    highest = lax.Precision.HIGHEST
    layers, lat_rows, lon_cols = displacement.shape
    lon_count = lax.axis_size("lon")
    lat_count = lax.axis_size("lat")
    total_lat = lat_rows * lat_count
    total_lon = lon_cols * lon_count
    layer_share = layers // lon_count
    stiff = lookup(materials, shear)
    restore = lookup(materials, restoring)
    rho_scale = lookup(materials, contrast)
    surface = (ice_mask.astype(jnp.float32) * ice_height)[None]
    load = jnp.concatenate(
        [surface, jnp.zeros((layers - 1, lat_rows, lon_cols), jnp.float32)], axis=0
    )
    lat_first = lax.axis_index("lat") * lat_rows
    theta = ((lat_first + jnp.arange(lat_rows)).astype(jnp.float32) + 0.5) * (jnp.pi / total_lat)
    table = legendre(theta)
    weights = jnp.sin(theta) / (4.0 * total_lat)
    own_columns = lax.axis_index("lon") * lon_cols + jnp.arange(lon_cols)
    layer_first = lax.axis_index("lon") * layer_share
    depth = 1
    for candidate in range(1, SWEEPS + 1):
        if SWEEPS % candidate == 0 and candidate <= min(lat_rows, lon_cols):
            depth = candidate
    forward, inverse = fourier_tables(own_columns, total_lon)
    field = displacement
    potential = jnp.zeros((layers, lat_rows, lon_cols), jnp.float32)
    for iteration in range(ITERS):
        force = load + potential
        field = margin_sweeps(field, force, stiff, restore, depth, lat_first, total_lat)
        density = rho_scale * field
        product = jnp.dot(
            density.reshape(layer_share * lax.axis_size("lon") * lat_rows, lon_cols),
            forward,
            precision=highest,
            preferred_element_type=jnp.float32,
        )
        spectrum = sum_at_owner(
            product.reshape(layer_share * lax.axis_size("lon"), lat_rows, 2 * LMAX), "lon", 0
        )
        weighted = spectrum.reshape(layer_share, lat_rows, 2, LMAX) * weights[None, :, None, None]
        coeffs = sum_at_owner(
            jnp.einsum("lam,kacm->lkcm", table, weighted, precision=highest), "lat", 0
        )
        green_part = lax.dynamic_slice_in_dim(green, layer_first, layer_share, 2)
        partial_pot = jnp.einsum("lkj,ljcm->lkcm", green_part, coeffs, precision=highest)
        pot_coeffs = sum_at_owner(partial_pot, "lon", 1)
        synth = jnp.einsum(
            "lam,lkcm->kacm", table, collect(pot_coeffs, "lat", 0), precision=highest
        )
        synth = synth.reshape(layer_share, lat_rows, 2 * LMAX)
        piece = collect(synth, "lon", 0)
        synth_product = jnp.dot(
            piece.reshape(piece.shape[0] * lat_rows, 2 * LMAX),
            inverse,
            precision=highest,
            preferred_element_type=jnp.float32,
        )
        potential = synth_product.reshape(piece.shape[0], lat_rows, lon_cols)
    return (field, potential)


def solution(mesh):
    in_specs = (
        P(None, "lat", "lon"),
        P(None, "lat", "lon"),
        P("lat", "lon"),
        P("lat", "lon"),
        P(),
        P(),
        P(),
        P("lat", None, None),
    )
    out_specs = (P(None, "lat", "lon"), P(None, "lat", "lon"))
    return jax.shard_map(
        on_device, mesh=mesh, in_specs=in_specs, out_specs=out_specs, check_vma=False
    )
```

profile of v0, /device:TPU:1, one launch (start us, length us, event | category | flops | bytes accessed | tf_op | source)
XLA Modules:
  0.0 1016.0 jit_solution(11613225863695073824)
XLA Ops:
  4.3 3.8 add_bitcast_fusion.1
  8.1 2.6 pad_bitcast_fusion
  11.0 5.5 collective-permute-start
  21.5 5.3 collective-permute-done.1
  27.9 2.1 fusion.206
  30.0 3.2 copy.28
  34.9 2.5 collective-permute-start.3
  38.7 3.6 collective-permute-done.2
  42.2 1.8 copy.30
  44.0 3.1 copy.31
  47.2 5.8 fusion.92
  53.7 1.7 fusion.107
  55.8 1.7 fusion.113
  59.9 3.3 fusion.174
  63.2 2.5 fusion.164
  65.8 8.0 all-to-all-start
  73.8 568.3 %while.19 = (s32[]{:T(128)}, f32[24,256]{1,0:T(8,128)S(1)}, f32[24,256]{1,0:T(8,128)S(1)}, f32[32,8,24,256]{3,2,1,0:T(8,128)}, s32[32,8]{0,1:T(8,128)S(1)}, /*in...) while((s32[]{:T(128)}, f32[24,256]{1,0:T(8,128)S(1)}, ...), condition=%wide.region_4.5_spmd.clone.clone, body=%wide.region_3.4_spmd.clone.clone.sunk | while | flops 1102778 | bytes 1254927 | solution.py:88
  642.1 6.6 copy.64
  649.4 6.3 convolution_bitcast_fusion.1
  657.0 2.4 copy.36
  659.4 13.6 %all-to-all-start.1 = ((f32[16,16,2,2,256]{4,1,3,2,0:T(8,128)}), f32[16,16,2,2,256]{4,1,3,2,0:T(8,128)S(1)}, u32[]{:S(2)}, u32[]{:S(2)}) async-start(f32[16,16,2,2,256]{4,1,3,2,0:T(8,128)} %copy.36), calls=%async_computation.1 | async-start | bytes 2097152 | tf_op jit(solution)/shard_map/all_to_all | solution.py:36
  673.0 27.4 %all-to-all-done.1 = f32[16,16,2,2,256]{4,1,3,2,0:T(8,128)S(1)} async-done(((f32[16,16,2,2,256]{4,1,3,2,0:T(8,128)}), f32[16,16,2,2,256]{4,1,3,2,0:T(8,128)S(1)}, u32[]{:S(2)}, u32[]{:S(2)}) %all-to-all-start.1) | async-done | bytes 1048608 | tf_op jit(solution)/shard_map/all_to_all | solution.py:36
  703.1 1.8 copy.89
  704.9 24.2 %all_to_all.50 = f32[16,16,2,2,256]{4,2,3,1,0:T(2,128)S(1)} all-to-all(f32[16,16,2,2,256]{4,2,3,1,0:T(2,128)S(1)} %bitcast.238), channel_id=1, replica_groups=mesh['lat'=16,'lon'=16] {'lon'}, dimensions={0} | all-to-all | bytes 2097152 | tf_op jit(solution)/shard_map/all_to_all | solution.py:36
  729.6 31.0 %all_to_all.51 = f32[16,16,2,2,256]{4,1,3,2,0:T(8,128)S(1)} all-to-all(f32[16,16,2,2,256]{4,1,3,2,0:T(8,128)S(1)} %broadcast_in_dim.507), channel_id=1, replica_groups=mesh['lat'=16,'lon'=16] {'lat'}, dimensions={0} | all-to-all | bytes 2097152 | tf_op jit(solution)/shard_map/all_to_all | solution.py:42
  763.3 7.5 convolution_bitcast_fusion.3
  771.4 27.7 %all_to_all.52 = f32[16,2,24,512]{3,2,1,0:T(8,128)S(1)} all-to-all(f32[16,2,24,512]{3,2,1,0:T(8,128)S(1)} %broadcast_in_dim.508), channel_id=1, replica_groups=mesh['lat'=16,'lon'=16] {'lon'}, dimensions={0} | all-to-all | bytes 3145728 | tf_op jit(solution)/shard_map/all_to_all | solution.py:42
  800.6 2.8 collective-permute-start.4
  804.8 2.9 collective-permute-done.4
  807.7 5.5 collective-permute-done.5
  814.3 2.2 fusion.205
  816.4 3.2 copy.46
  819.7 2.6 collective-permute-start.6
  825.9 1.8 copy.48
  827.7 2.7 collective-permute-done.7
  830.3 3.2 copy.49
  833.5 5.6 fusion.96
  839.8 1.7 fusion.125
  841.9 1.7 fusion.131
  846.1 4.1 fusion.173
  851.5 28.4 %all_to_all.53 = f32[16,2,24,512]{3,2,1,0:T(8,128)S(1)} all-to-all(f32[16,2,24,512]{3,2,1,0:T(8,128)S(1)} %fusion.162), channel_id=1, replica_groups=mesh['lat'=16,'lon'=16] {'lon'}, dimensions={0} | all-to-all | bytes 3145728 | tf_op jit(solution)/shard_map/all_to_all | solution.py:36
  880.5 6.3 convolution_bitcast_fusion
  887.5 34.2 %all_to_all.54 = f32[16,16,2,2,256]{4,1,3,2,0:T(8,128)S(1)} all-to-all(f32[16,16,2,2,256]{4,1,3,2,0:T(8,128)S(1)} %copy.53), channel_id=1, replica_groups=mesh['lat'=16,'lon'=16] {'lat'}, dimensions={0} | all-to-all | bytes 2097152 | tf_op jit(solution)/shard_map/all_to_all | solution.py:36
  924.0 21.9 %all_to_all.55 = f32[16,16,2,2,256]{4,2,3,1,0:T(2,128)S(1)} all-to-all(f32[16,16,2,2,256]{4,2,3,1,0:T(2,128)S(1)} %bitcast.241), channel_id=1, replica_groups=mesh['lat'=16,'lon'=16] {'lon'}, dimensions={0} | all-to-all | bytes 2097152 | tf_op jit(solution)/shard_map/all_to_all | solution.py:36
  946.4 30.8 %all_to_all.56 = f32[16,16,2,2,256]{4,1,3,2,0:T(8,128)S(1)} all-to-all(f32[16,16,2,2,256]{4,1,3,2,0:T(8,128)S(1)} %broadcast_in_dim.509), channel_id=1, replica_groups=mesh['lat'=16,'lon'=16] {'lat'}, dimensions={0} | all-to-all | bytes 2097152 | tf_op jit(solution)/shard_map/all_to_all | solution.py:42
  977.9 7.5 convolution_bitcast_fusion.2
  986.0 27.6 %all_to_all.57 = f32[16,2,24,512]{3,2,1,0:T(8,128)S(1)} all-to-all(f32[16,2,24,512]{3,2,1,0:T(8,128)S(1)} %broadcast_in_dim.510), channel_id=1, replica_groups=mesh['lat'=16,'lon'=16] {'lon'}, dimensions={0} | all-to-all | bytes 3145728 | tf_op jit(solution)/shard_map/all_to_all | solution.py:42
  1013.6 2.1 fusion.166
  (1476 shorter events, 285.6 us)
Async XLA Ops:
  0.6 699.9 %copy-start = (f32[16,32,32]{2,1,0:T(8,128)S(1)}, f32[16,32,32]{2,1,0:T(8,128)}, u32[]{:S(2)}) copy-start(f32[16,32,32]{2,1,0:T(8,128)} %param.17) | copy-start | bytes 196612
  0.6 10.1 copy-start.4
  8.0 2.7 copy-start.5
  8.1 2.7 copy-start.8
  8.1 2.7 copy-start.11
  8.1 2.7 copy-start.14
  10.7 16.1 %copy-start.2 = (f32[1,32,24,128]{3,2,1,0:T(8,128)}, f32[1,32,24,128]{3,2,1,0:T(8,128)S(1)}, u32[]{:S(2)}) copy-start(f32[1,32,24,128]{3,2,1,0:T(8,128)S(1)} %get-tuple-element.515) | copy-start | bytes 1179652
  10.8 8.0 copy-start.21
  11.0 10.4 %collective-permute-start = (f32[4,32,4,128]{3,2,1,0:T(4,128)S(1)}, f32[4,32,4,128]{3,2,1,0:T(4,128)S(1)}, u32[]{:S(2)}, u32[]{:S(2)}) collective-permute-start(f32[4,32,4,128]{3,2,1,0:T(4,128)S(1)} %get-tuple-element.499), channel_id=1, source_target_pairs={{0,16},{16,32},{32,48},{48,64},{64,80},{80,96},{96,112},{112,128},... | collective-permute-start | bytes 786440 | tf_op jit(solution)/shard_map/ppermute | solution.py:20
  16.5 10.3 %collective-permute-start.1 = (f32[4,32,4,128]{3,2,1,0:T(4,128)S(1)}, f32[4,32,4,128]{3,2,1,0:T(4,128)S(1)}, u32[]{:S(2)}, u32[]{:S(2)}) collective-permute-start(f32[4,32,4,128]{3,2,1,0:T(4,128)S(1)} %get-tuple-element.500), channel_id=1, source_target_pairs={{16,0},{32,16},{48,32},{64,48},{80,64},{96,80},{112,96},{128,112},... | collective-permute-start | bytes 786440 | tf_op jit(solution)/shard_map/ppermute | solution.py:22
  21.5 5.4 copy-start.17
  26.8 0.7 copy-start.18
  34.9 9.1 collective-permute-start.3
  37.4 4.8 collective-permute-start.2
  57.9 2.0 copy-start.6
  57.9 2.0 copy-start.9
  57.9 2.0 copy-start.12
  57.9 2.0 copy-start.15
  63.2 749.9 %copy-start.1 = (f32[32,24,128]{2,1,0:T(8,128)}, f32[32,24,128]{2,1,0:T(8,128)S(1)}, u32[]{:S(2)}) copy-start(f32[32,24,128]{2,1,0:T(8,128)S(1)} %get-tuple-element.449) | copy-start | bytes 1179652
  65.8 583.0 %all-to-all-start = ((f32[16,2,24,512]{3,2,1,0:T(8,128)}), f32[16,2,24,512]{3,2,1,0:T(8,128)S(1)}, u32[]{:S(2)}, u32[]{:S(2)}) async-start(f32[16,2,24,512]{3,2,1,0:T(8,128)} %fusion.164), calls=%async_computation | async-start | bytes 3145728 | tf_op jit(solution)/shard_map/all_to_all | solution.py:36
  659.4 41.0 %all-to-all-start.1 = ((f32[16,16,2,2,256]{4,1,3,2,0:T(8,128)}), f32[16,16,2,2,256]{4,1,3,2,0:T(8,128)S(1)}, u32[]{:S(2)}, u32[]{:S(2)}) async-start(f32[16,16,2,2,256]{4,1,3,2,0:T(8,128)} %copy.36), calls=%async_computation.1 | async-start | bytes 2097152 | tf_op jit(solution)/shard_map/all_to_all | solution.py:36
  800.4 12.8 %copy-start.3 = (f32[1,32,24,128]{3,2,1,0:T(8,128)}, f32[1,32,24,128]{3,2,1,0:T(8,128)S(1)}, u32[]{:S(2)}) copy-start(f32[1,32,24,128]{3,2,1,0:T(8,128)S(1)} %fusion.101) | copy-start | bytes 1179652
  800.6 7.0 collective-permute-start.4
  803.5 9.7 collective-permute-start.5
  807.7 5.5 copy-start.19
  813.2 0.7 copy-start.20
  819.7 6.2 collective-permute-start.6
  823.9 6.4 collective-permute-start.7
  844.0 2.0 copy-start.7
  844.1 2.0 copy-start.10
  844.1 2.0 copy-start.13
  844.1 2.0 copy-start.16
where the time goes:
time: 1030 us; the launch traced here: 1020 us
  loops' own time  325 us (32%)
  other arithmetic  239 us (23%)
  blocking collectives  226 us (22%)
  local copies, waits for them, and re-layouts  98.2 us (10%)
  waiting for transfers between devices  50.3 us (5%)
  starting transfers between devices  39.3 us (4%)
  matrix products  37 us (4%)
    another operation x1, loops' own time, legendre(): _, table = lax.scan(advance, (zeros, zeros), jnp.arange(LMAX), unroll=8)  325 us
    eq x160, other arithmetic, advance(): orders == degree  159 us
    all_to_all x4, blocking collectives, from_everyone(): return lax.all_to_all(copies, axis, split_axis=0, concat_axis=0, tiled=True)  117 us
    all_to_all x4, blocking collectives, sum_at_owner(): lax.all_to_all(split_up(array, dim, devices), axis, 0, 0, tiled=True)  109 us
    all_to_all x2, waiting for transfers between devices, sum_at_owner(): lax.all_to_all(split_up(array, dim, devices), axis, 0, 0, tiled=True)  27.4 us
    while x224, other arithmetic  23.8 us
    dynamic_update_slice x32, local copies, waits for them, and re-layouts, legendre(): _, table = lax.scan(advance, (zeros, zeros), jnp.arange(LMAX), unroll=8)  22.4 us
    all_to_all x2, starting transfers between devices, sum_at_owner(): lax.all_to_all(split_up(array, dim, devices), axis, 0, 0, tiled=True)  21.6 us
  transfers between devices with their start and end apart: 10, of which 8 were waited for; matrix products, arithmetic and copies ran while one was open for 25% of the time, Pallas kernels for 0%

commit v1 on v0

v1 whole, which is shorter than its diff:
```python
import functools
import math

import jax
import jax.numpy as jnp
from jax import lax
from jax.experimental import pallas as pl
from jax.experimental.pallas import tpu as pltpu
from jax.sharding import PartitionSpec as P

L = 32
LMAX = 256
NLAT = 384
NLON = 2048
SWEEPS = 4
N = 16
ROWS = 24
COLS = 128
F32 = jnp.float32
BF16 = jnp.bfloat16
MESH = pl.DeviceIdType.MESH


def iota(shape, dim):
    return lax.broadcasted_iota(jnp.int32, shape, dim)


def split(x):
    hi = x.astype(BF16)
    lo = (x - hi.astype(F32)).astype(BF16)
    return hi, lo


def dot(a, b):
    return jnp.dot(a, b, preferred_element_type=F32)


def dot_t(a, b):
    return lax.dot_general(a, b, (((1,), (1,)), ((), ())), preferred_element_type=F32)


def lookup(mat, table):
    out = jnp.where(mat == 0, table[0], 0.0)
    for material in range(1, 4):
        out = jnp.where(mat == material, table[material], out)
    return out


def kernel(
    u_in,
    mat_in,
    mask_in,
    ice_in,
    shear,
    restoring,
    contrast,
    green_in,
    u_out,
    pot_out,
    U,
    Bc,
    Rd,
    Ac,
    rho,
    dens,
    R1,
    FH,
    FL,
    WH,
    WL,
    C16,
    S16,
    wrow,
    Z,
    T2,
    R2,
    AH,
    C3,
    T3,
    R3,
    T4,
    R4,
    XH,
    Y,
    T5,
    R5,
    X5,
    T6,
    R6,
    GR,
    Pf,
    Ph,
    Pl,
    matf,
    load,
    loadx,
    E,
    EL,
    ER,
    PK,
    VT,
    VB,
    WT,
    WB,
    send_sem,
    recv_sem,
    hsend,
    hrecv,
    gsem,
):
    me_lat = lax.axis_index("lat")
    me_lon = lax.axis_index("lon")

    barrier = pltpu.get_barrier_semaphore()

    def greet(d, carry):
        pl.semaphore_signal(barrier, inc=1, device_id={"lon": lax.rem(me_lon + d, N)}, device_id_type=MESH)
        pl.semaphore_signal(barrier, inc=1, device_id={"lat": lax.rem(me_lat + d, N)}, device_id_type=MESH)
        return carry

    lax.fori_loop(1, N, greet, 0)
    pl.semaphore_signal(
        barrier, inc=1, device_id={"lat": me_lon, "lon": lax.rem(me_lat + 1, N)}, device_id_type=MESH
    )

    def tables():
        q = iota((COLS, LMAX), 0)
        m = iota((COLS, LMAX), 1)
        angle = (2.0 * math.pi / NLON) * ((q * m) & (NLON - 1)).astype(F32)
        hi, lo = split(jnp.cos(angle))
        FH[:, 0:LMAX] = hi
        FL[:, 0:LMAX] = lo
        hi, lo = split(jnp.sin(angle))
        FH[:, LMAX:] = hi
        FL[:, LMAX:] = lo
        p = iota((N, LMAX), 0)
        m = iota((N, LMAX), 1)
        angle = (2.0 * math.pi / N) * ((p * m) & (N - 1)).astype(F32)
        C16[...] = jnp.cos(angle)
        S16[...] = jnp.sin(angle)
        lane = iota((LMAX, 2 * COLS), 1)
        m = iota((LMAX, 2 * COLS), 0)
        q = jnp.where(lane < 128, lane, jnp.where(lane < 132, lane - 132 + NLON, lane - 4))
        angle = (2.0 * math.pi / NLON) * ((q * m) & (NLON - 1)).astype(F32)
        hi, lo = split(jnp.cos(angle))
        WH[0:LMAX, :] = hi
        WL[0:LMAX, :] = lo
        hi, lo = split(jnp.sin(angle))
        WH[LMAX:, :] = hi
        WL[LMAX:, :] = lo
        row = iota((ROWS, LMAX), 0) + me_lat * ROWS
        w = jnp.sin((row.astype(F32) + 0.5) * (math.pi / NLAT)) * (2.0 * math.pi / NLON / (4.0 * NLAT))
        wrow[0:ROWS, :] = w
        wrow[ROWS:, :] = w
        Z[...] = jnp.zeros_like(Z)
        C3[...] = jnp.zeros_like(C3)
        for b in range(2):
            U[b, 0] = jnp.zeros((32, 256), F32)
            U[b, L + 1] = jnp.zeros((32, 256), F32)

    def prepare():
        def one(k, carry):
            mat = mat_in[k]
            matf[k] = mat.astype(F32)
            rho[k] = lookup(mat, contrast)
            return carry

        lax.fori_loop(0, L, one, 0)
        load[...] = mask_in[...].astype(F32) * ice_in[...]

    lane24 = iota((ROWS, COLS), 1)

    def pack(read, g):
        def one(kk, acc):
            return jnp.where(lane24 // 8 == kk, pltpu.roll(read(16 * g + kk), 8 * kk + 4, 1), acc)

        return lax.fori_loop(0, 16, one, jnp.zeros((ROWS, COLS), F32))

    left = lax.rem(me_lon + N - 1, N)
    right = lax.rem(me_lon + 1, N)
    up = lax.rem(me_lat + N - 1, N)
    down = lax.rem(me_lat + 1, N)

    def edge_copies(it):
        first, count = (0, 5) if it == 0 else (5, 2)
        part = pl.ds(first, count)
        return [
            pltpu.make_async_remote_copy(
                E.at[part], ER.at[part], hsend.at[it, 0], hrecv.at[it, 0], device_id={"lon": left}, device_id_type=MESH
            ),
            pltpu.make_async_remote_copy(
                E.at[part], EL.at[part], hsend.at[it, 1], hrecv.at[it, 1], device_id={"lon": right}, device_id_type=MESH
            ),
        ]

    def row_copies(it):
        first, count = (0, 35) if it == 0 else (35, 17)
        part = pl.ds(first, count)
        return [
            pltpu.make_async_remote_copy(
                VT.at[part], WT.at[part], hsend.at[it, 2], hrecv.at[it, 2], device_id={"lat": up}, device_id_type=MESH
            ),
            pltpu.make_async_remote_copy(
                VB.at[part], WB.at[part], hsend.at[it, 3], hrecv.at[it, 3], device_id={"lat": down}, device_id_type=MESH
            ),
        ]

    def merge_edges(it):
        first, count = (0, 5) if it == 0 else (5, 2)
        for g in range(count):
            PK[g, 0:ROWS] = jnp.where(lane24 % 8 < 4, EL[first + g], ER[first + g])

    row8 = iota((8, COLS), 0)

    def pair_rows(t, a_top, a_bot, b_top, b_bot):
        VT[t] = jnp.where(row8 < 4, a_top, pltpu.roll(b_top, 4, 0))
        VB[t] = jnp.where(row8 < 4, pltpu.roll(a_bot, 4, 0), b_bot)

    def halo_rows(t):
        top, bot = WT[t], WB[t]
        first = jnp.where(row8 < 4, top, pltpu.roll(bot, 4, 0))
        second = jnp.where(row8 < 4, pltpu.roll(top, 4, 0), bot)
        return first, second

    rows32 = iota((32, 256), 0)
    global_row = me_lat * ROWS + jnp.where(rows32 < 28, rows32, rows32 - 32)
    inside = (global_row >= 0) & (global_row < NLAT)
    inside8 = inside[24:32, 0:COLS]

    def pair_u(base):
        def one(k, carry):
            pair_rows(
                base + k,
                U[0, k + 1, 0:8, 0:COLS],
                U[0, k + 1, 16:24, 0:COLS],
                U[0, k + 17, 0:8, 0:COLS],
                U[0, k + 17, 16:24, 0:COLS],
            )
            return carry

        lax.fori_loop(0, 16, one, 0)
        pair_rows(base + 16, PK[0, 0:8], PK[0, 16:24], PK[1, 0:8], PK[1, 16:24])

    def fill_u(base):
        first, second = halo_rows(base + 16)
        PK[0, 24:32] = jnp.where(inside8, first, 0.0)
        PK[1, 24:32] = jnp.where(inside8, second, 0.0)

        def one(k, carry):
            first, second = halo_rows(base + k)
            U[0, k + 1, 24:32, 0:COLS] = jnp.where(inside8, first, 0.0)
            U[0, k + 17, 24:32, 0:COLS] = jnp.where(inside8, second, 0.0)
            U[0, k + 1, :, COLS:] = pltpu.roll(PK[0], 124 - 8 * k, 1)
            U[0, k + 17, :, COLS:] = pltpu.roll(PK[1], 124 - 8 * k, 1)
            return carry

        lax.fori_loop(0, 16, one, 0)

    def legendre():
        lane = iota((N, 512), 1)
        order = (iota((N, 512), 0) + me_lat * N).astype(F32)
        aa = lane % 32
        a = (lane // 32) * ROWS + jnp.where(aa < 28, aa, aa - 32)
        a = jnp.clip(a, 0, NLAT - 1)
        theta = (a.astype(F32) + 0.5) * (math.pi / NLAT)
        cosine = jnp.cos(theta)
        sine = jnp.sin(theta)
        t = iota((N, LMAX), 1)
        m_int = iota((N, LMAX), 0) + me_lat * N
        t_f = jnp.maximum(t.astype(F32), 1.0)
        growth = jnp.where((t >= 2) & (t <= m_int), 0.5 * jnp.log((2.0 * t_f + 1.0) / (2.0 * t_f)), 0.0)
        log_diag = jnp.sum(growth, axis=1, keepdims=True) + 0.5 * math.log(3.0)
        log_diag = jnp.where(m_int[:, 0:1] >= 1, log_diag, 0.0)
        diagonal = jnp.exp(log_diag + order * jnp.log(sine))
        start = jnp.sqrt(2.0 * order + 3.0) * cosine * diagonal
        deg = iota((N, LMAX), 1).astype(F32)
        m_f = m_int.astype(F32)
        first = jnp.sqrt(
            jnp.maximum(4.0 * deg * deg - 1.0, 1.0) / jnp.maximum(deg * deg - m_f * m_f, 1.0)
        )
        second = jnp.sqrt(
            jnp.maximum((deg - 1.0) * (deg - 1.0) - m_f * m_f, 0.0)
            / jnp.maximum(4.0 * (deg - 1.0) * (deg - 1.0) - 1.0, 1.0)
        )
        order_i = iota((N, 512), 0) + me_lat * N

        def block(lb, carry):
            one, two = carry
            shift = lax.rem(LMAX - 8 * lb, LMAX)
            f = pltpu.roll(first, shift, 1)[:, 0:COLS]
            s = pltpu.roll(second, shift, 1)[:, 0:COLS]
            for r in range(8):
                degree = lb * 8 + r
                fb = jnp.broadcast_to(f[:, r : r + 1], (N, 512))
                sb = jnp.broadcast_to(s[:, r : r + 1], (N, 512))
                general = fb * (cosine * one - sb * two)
                value = jnp.where(
                    order_i == degree, diagonal, jnp.where(order_i == degree - 1, start, general)
                )
                for tile in range(4):
                    Pf[tile, pl.ds(pl.multiple_of(degree * N, N), N), :] = value[:, tile * COLS : (tile + 1) * COLS]
                one, two = value, one
            return one, two

        zeros = jnp.zeros((N, 512), F32)
        lax.fori_loop(0, LMAX // 8, block, (zeros, zeros))

    def legendre_split():
        def one(m, carry):
            for tile in range(4):
                value = Pf[tile, pl.ds(m, LMAX, stride=N), :]
                hi, lo = split(value)
                Ph[m, :, tile * COLS : (tile + 1) * COLS] = hi
                Pl[m, :, tile * COLS : (tile + 1) * COLS] = lo
            return carry

        lax.fori_loop(0, N, one, 0)

    def exchange(phase, axis, src, dst, peer, sender):
        return pltpu.make_async_remote_copy(
            src,
            dst,
            send_sem.at[phase, peer],
            recv_sem.at[phase, sender],
            device_id={axis: peer},
            device_id_type=MESH,
        )

    def slab(ref, index):
        return ref.at[pl.ds(pl.multiple_of(index * N, N), N)]

    def swap_start(phase, axis, me, src, dst):
        def one(d, carry):
            peer = lax.rem(me + d, N)
            exchange(phase, axis, slab(src, peer), slab(dst, me), peer, me).start()
            return carry

        lax.fori_loop(1, N, one, 0)
        mine = pl.ds(pl.multiple_of(me * N, N), N)
        dst[mine, :] = src[mine, :]

    def swap_wait(phase, axis, me, src, dst):
        def one(d, carry):
            peer = lax.rem(me + d, N)
            copy = exchange(phase, axis, slab(src, peer), slab(dst, peer), peer, peer)
            copy.wait_send()
            copy.wait_recv()
            return carry

        lax.fori_loop(1, N, one, 0)

    def sweep(src, dst):
        def one(k, carry):
            c = U[src, k + 1]
            around = (
                pltpu.roll(c, 1, 0)
                + pltpu.roll(c, 31, 0)
                + pltpu.roll(c, 1, 1)
                + pltpu.roll(c, 255, 1)
                + U[src, k]
                + U[src, k + 2]
            )
            U[dst, k + 1] = Ac[k] + Bc[k] * around
            return carry

        lax.fori_loop(0, L, one, 0)

    def coefficients():
        first, second = halo_rows(33)
        PK[2, 24:32] = first
        PK[3, 24:32] = second

        def one(k, carry):
            low = []
            first, second = halo_rows(17 + k)
            for kk, rows in ((k, first), (k + 16, second)):
                g = 2 if len(low) == 0 else 3
                low.append(g)
                main = jnp.concatenate([matf[kk], rows], axis=0)
                side = pltpu.roll(PK[g], 124 - 8 * k, 1)
                mat = jnp.concatenate([main, side], axis=1)
                st = lookup(mat, shear)
                re = lookup(mat, restoring)
                inv = jnp.where(inside, 1.0 / (6.0 * st + re), 0.0)
                Rd[kk] = inv
                Bc[kk] = st * inv
                Ac[kk] = jnp.zeros((32, 256), F32)
            return carry

        lax.fori_loop(0, 16, one, 0)
        first, second = halo_rows(34)
        PK[4, 24:32] = second
        loadx[0:ROWS, 0:COLS] = load[...]
        loadx[ROWS:, 0:COLS] = first
        loadx[:, COLS:] = pltpu.roll(PK[4], 124, 1)
        Ac[0] = loadx[...] * Rd[0]

    lane16 = iota((N, COLS), 1)
    rowmod = iota((64, LMAX), 0) % N
    rowmod_w = iota((64, 512), 0) % N

    def forward_fourier():
        def part(p, acc):
            acc_c, acc_s = acc
            x = R1[p].reshape(2 * ROWS, COLS)
            hi, lo = split(x)
            r = dot(jnp.concatenate([hi, lo], axis=0), FH[...])
            r = r[0 : 2 * ROWS] + r[2 * ROWS :] + dot(hi, FL[...])
            yc = r[:, 0:LMAX]
            ys = r[:, LMAX:]
            c = C16[pl.ds(p, 1), :]
            s = S16[pl.ds(p, 1), :]
            return acc_c + (c * yc - s * ys), acc_s + (s * yc + c * ys)

        def one(d, acc):
            p = lax.rem(me_lon + d, N)
            copy = exchange(0, "lon", dens.at[p], R1.at[p], p, p)
            copy.wait_send()
            copy.wait_recv()
            return part(p, acc)

        zeros = jnp.zeros((2 * ROWS, LMAX), F32)
        R1[me_lon] = dens[me_lon]
        acc_c, acc_s = lax.fori_loop(1, N, one, part(me_lon, (zeros, zeros)))
        for c, acc in ((0, acc_c), (1, acc_s)):
            acc = acc * wrow[...]
            for kk in range(2):
                Z[(2 * c + kk) * 32 : (2 * c + kk) * 32 + ROWS, :] = acc[kk * ROWS : (kk + 1) * ROWS]
        T2[...] = jnp.transpose(Z[...])

    def forward_legendre():
        for t in range(4):
            parts = [R2[(4 * t + ii) * N : (4 * t + ii + 1) * N, :] for ii in range(4)]
            for ck in range(4):
                out = None
                for ii in range(4):
                    turn = ((ii - ck) * 32) % COLS
                    v = parts[ii] if turn == 0 else pltpu.roll(parts[ii], turn, 1)
                    out = v if out is None else jnp.where(lane16 // 32 == ii, v, out)
                hi, lo = split(out)
                AH[ck * N : (ck + 1) * N, t * COLS : (t + 1) * COLS] = hi
                AH[64 + ck * N : 64 + (ck + 1) * N, t * COLS : (t + 1) * COLS] = lo

        def one(m, acc):
            r = dot_t(AH[...], Ph[m])
            r = r[0:64] + r[64:] + dot_t(AH[0:64], Pl[m])
            return jnp.where(rowmod == m, r, acc)

        C3[0:64, :] = lax.fori_loop(0, N, one, jnp.zeros((64, LMAX), F32))
        T3[...] = jnp.transpose(C3[...])

    def layer_sum():
        even = (lane16 // 16) % 2 == 0
        for l in range(N):
            r = R3[pl.ds(l, N, stride=N), :]
            r = jnp.concatenate([r, pltpu.roll(r, COLS - 16, 1)], axis=0)
            out = jnp.dot(GR[l], r, precision=lax.Precision.HIGHEST, preferred_element_type=F32)
            T4[pl.ds(l, N, stride=N), :] = jnp.where(even, out[0:N], pltpu.roll(out[N:], 16, 1))

    def inverse_legendre():
        hi, lo = split(jnp.transpose(R4[...])[0:64])
        XH[0:64, :] = hi
        XH[64:, :] = lo

        def one(m, carry):
            r = dot(XH[...], Ph[m])
            r = r[0:64] + r[64:] + dot(XH[0:64], Pl[m])
            Y[...] = jnp.where(rowmod_w == m, r, Y[...])
            return carry

        Y[...] = jnp.zeros_like(Y)
        lax.fori_loop(0, N, one, 0)
        for i in range(N):
            t, ii = i // 4, i % 4
            out = None
            for ck in range(4):
                turn = ((ck - ii) * 32) % COLS
                v = Y[ck * N : (ck + 1) * N, t * COLS : (t + 1) * COLS]
                v = v if turn == 0 else pltpu.roll(v, turn, 1)
                out = v if out is None else jnp.where(lane16 // 32 == ck, v, out)
            T5[i * N : (i + 1) * N, :] = out

    lane8 = iota((8, COLS), 1)

    def inverse_fourier():
        X5[...] = jnp.transpose(R5[...])

        def one(d, carry):
            p = lax.rem(me_lon + d, N)
            c = C16[pl.ds(p, 1), :]
            s = S16[pl.ds(p, 1), :]
            a = X5[0:64, :]
            b = X5[64:, :]
            x = jnp.concatenate([a * c + b * s, b * c - a * s], axis=1)
            hi, lo = split(x)
            r = dot(jnp.concatenate([hi, lo], axis=0), WH[...])
            r = r[0:64] + r[64:] + dot(hi, WL[...])
            T6[p, 0:64, :] = r[:, 0:COLS]
            side = r[0:8, COLS:]
            for t in range(1, 8):
                side = jnp.where(lane8 // 8 == t, pltpu.roll(r[8 * t : 8 * t + 8, COLS:], 8 * t, 1), side)
            T6[p, 64:72, :] = side

            @pl.when(d < N)
            def _():
                exchange(5, "lon", T6.at[p], R6.at[me_lon], p, me_lon).start()

            return carry

        lax.fori_loop(1, N + 1, one, 0)
        R6[me_lon] = T6[me_lon]

        def wait(d, carry):
            p = lax.rem(me_lon + d, N)
            copy = exchange(5, "lon", T6.at[p], R6.at[p], p, p)
            copy.wait_send()
            copy.wait_recv()
            return carry

        lax.fori_loop(1, N, wait, 0)

    def send_density():
        def one(q, carry):
            for kk in range(2):
                k = kk * N + q
                dens[q, kk] = rho[k] * U[0, k + 1, 0:ROWS, 0:COLS]
            return carry

        lax.fori_loop(0, N, one, 0)

        def start(d, carry):
            p = lax.rem(me_lon + d, N)
            exchange(0, "lon", dens.at[p], R1.at[me_lon], p, me_lon).start()
            return carry

        lax.fori_loop(1, N, start, 0)

    def load_u(k, carry):
        U[0, k + 1, 0:ROWS, 0:COLS] = u_in[k]
        return carry

    prepare()
    lax.fori_loop(0, L, load_u, 0)
    E[0] = pack(lambda k: u_in[k], 0)
    E[1] = pack(lambda k: u_in[k], 1)
    E[2] = pack(lambda k: matf[k], 0)
    E[3] = pack(lambda k: matf[k], 1)
    E[4] = pltpu.roll(load[...], 4, 1)
    pl.semaphore_wait(barrier, 2 * N - 1)
    edges = edge_copies(0)
    for copy in edges:
        copy.start()
    tables()
    for copy in edges:
        copy.wait()
    merge_edges(0)
    pair_u(0)

    def pair_mat(k, carry):
        pair_rows(17 + k, matf[k, 0:8], matf[k, 16:24], matf[k + 16, 0:8], matf[k + 16, 16:24])
        return carry

    lax.fori_loop(0, 16, pair_mat, 0)
    pair_rows(33, PK[2, 0:8], PK[2, 16:24], PK[3, 0:8], PK[3, 16:24])
    pair_rows(34, load[0:8], load[16:24], PK[4, 0:8], PK[4, 16:24])
    rows = row_copies(0)
    for copy in rows:
        copy.start()
    green = pltpu.make_async_remote_copy(
        green_in,
        GR,
        gsem.at[0],
        gsem.at[1],
        device_id={"lat": lax.rem(me_lon + N - 1, N), "lon": me_lat},
        device_id_type=MESH,
    )
    green.start()
    legendre()
    legendre_split()
    for copy in rows:
        copy.wait()
    fill_u(0)
    coefficients()

    for it in range(2):
        if it == 1:
            for copy in rows:
                copy.wait()
            fill_u(35)

            def force(j, carry):
                side = R6[j, 64:72, :]
                for kk in range(2):
                    k = kk * N + j
                    main = R6[j, kk * 32 : (kk + 1) * 32, :]
                    halo = jnp.concatenate(
                        [pltpu.roll(side, 124 - 8 * (4 * kk + g), 1) for g in range(4)], axis=0
                    )
                    Ac[k] = jnp.concatenate([main, halo], axis=1) * Rd[k]
                return carry

            lax.fori_loop(0, N, force, 0)
            Ac[0] = Ac[0] + loadx[...] * Rd[0]
        for s in range(SWEEPS):
            sweep(s % 2, (s + 1) % 2)
        send_density()
        if it == 0:
            E[5] = pack(lambda k: U[0, k + 1, 0:ROWS, 0:COLS], 0)
            E[6] = pack(lambda k: U[0, k + 1, 0:ROWS, 0:COLS], 1)
        else:

            def store_u(k, carry):
                u_out[k] = U[0, k + 1, 0:ROWS, 0:COLS]
                return carry

            lax.fori_loop(0, L, store_u, 0)
        forward_fourier()
        swap_start(1, "lat", me_lat, T2, R2)
        if it == 0:
            edges = edge_copies(1)
            for copy in edges:
                copy.start()
        swap_wait(1, "lat", me_lat, T2, R2)
        forward_legendre()
        swap_start(2, "lon", me_lon, T3, R3)
        if it == 0:
            for copy in edges:
                copy.wait()
            merge_edges(1)
            pair_u(35)
            rows = row_copies(1)
            for copy in rows:
                copy.start()
            green.wait()
        swap_wait(2, "lon", me_lon, T3, R3)
        layer_sum()
        swap_start(3, "lon", me_lon, T4, R4)
        swap_wait(3, "lon", me_lon, T4, R4)
        inverse_legendre()
        swap_start(4, "lat", me_lat, T5, R5)
        swap_wait(4, "lat", me_lat, T5, R5)
        inverse_fourier()

    def store_pot(j, carry):
        for kk in range(2):
            pot_out[kk * N + j] = R6[j, kk * 32 : kk * 32 + ROWS, :]
        return carry

    lax.fori_loop(0, N, store_pot, 0)


def on_device(displacement, materials, ice_mask, ice_height, shear, restoring, contrast, green):
    vmem = pl.BlockSpec(memory_space=pltpu.VMEM)
    smem = pl.BlockSpec(memory_space=pltpu.SMEM)
    field = jax.ShapeDtypeStruct((L, ROWS, COLS), F32)
    scratch = [
        ((2, L + 2, 32, 256), F32),
        ((L, 32, 256), F32),
        ((L, 32, 256), F32),
        ((L, 32, 256), F32),
        ((L, ROWS, COLS), F32),
        ((N, 2, ROWS, COLS), F32),
        ((N, 2, ROWS, COLS), F32),
        ((COLS, 512), BF16),
        ((COLS, 512), BF16),
        ((512, 256), BF16),
        ((512, 256), BF16),
        ((N, LMAX), F32),
        ((N, LMAX), F32),
        ((2 * ROWS, LMAX), F32),
        ((128, LMAX), F32),
        ((LMAX, COLS), F32),
        ((LMAX, COLS), F32),
        ((128, 512), BF16),
        ((128, LMAX), F32),
        ((LMAX, COLS), F32),
        ((LMAX, COLS), F32),
        ((LMAX, COLS), F32),
        ((LMAX, COLS), F32),
        ((128, LMAX), BF16),
        ((64, 512), F32),
        ((LMAX, COLS), F32),
        ((LMAX, COLS), F32),
        ((128, LMAX), F32),
        ((N, 72, COLS), F32),
        ((N, 72, COLS), F32),
        ((N, L, L), F32),
        ((4, LMAX * N, COLS), F32),
        ((N, LMAX, 512), BF16),
        ((N, LMAX, 512), BF16),
        ((L, ROWS, COLS), F32),
        ((ROWS, COLS), F32),
        ((32, 256), F32),
        ((7, ROWS, COLS), F32),
        ((7, ROWS, COLS), F32),
        ((7, ROWS, COLS), F32),
        ((5, 32, COLS), F32),
        ((52, 8, COLS), F32),
        ((52, 8, COLS), F32),
        ((52, 8, COLS), F32),
        ((52, 8, COLS), F32),
    ]
    return pl.pallas_call(
        kernel,
        out_shape=(field, field),
        in_specs=[vmem] * 4 + [smem] * 3 + [vmem],
        out_specs=(vmem, vmem),
        scratch_shapes=[pltpu.VMEM(shape, dtype) for shape, dtype in scratch]
        + [
            pltpu.SemaphoreType.DMA((6, N)),
            pltpu.SemaphoreType.DMA((6, N)),
            pltpu.SemaphoreType.DMA((2, 4)),
            pltpu.SemaphoreType.DMA((2, 4)),
            pltpu.SemaphoreType.DMA((2,)),
        ],
        compiler_params=pltpu.CompilerParams(
            collective_id=0, has_side_effects=True, vmem_limit_bytes=60 * 1024 * 1024
        ),
    )(displacement, materials, ice_mask, ice_height, shear, restoring, contrast, green)


def solution(mesh):
    in_specs = (
        P(None, "lat", "lon"),
        P(None, "lat", "lon"),
        P("lat", "lon"),
        P("lat", "lon"),
        P(),
        P(),
        P(),
        P("lat", None, None),
    )
    out_specs = (P(None, "lat", "lon"), P(None, "lat", "lon"))
    return jax.shard_map(
        on_device, mesh=mesh, in_specs=in_specs, out_specs=out_specs, check_vma=False
    )
```

time: 1030 us -> 173 us (0.17); the launches traced: 1020 us -> 173 us
  loops' own time: 325 us -> 0 us
  other arithmetic: 239 us -> 0 us
  blocking collectives: 226 us -> 0 us
  Pallas kernels: 0 us -> 170 us
  local copies, waits for them, and re-layouts: 98.2 us -> 2.57 us
  waiting for transfers between devices: 50.3 us -> 0 us
  starting transfers between devices: 39.3 us -> 0 us
  matrix products: 37 us -> 0 us
    another operation x1 -> x0, loops' own time: 325 us -> none  [legendre(): _, table = lax.scan(advance, (zeros, zeros), jnp.arange(LMAX), unroll=8)]
    all_to_all x8 -> x0, blocking collectives: 226 us -> none  [the longest x4 117 us: from_everyone(): return lax.all_to_all(copies, axis, split_axis=0, concat_axis=0, tiled=True)]
    pallas_call x0 -> x1, Pallas kernels: none -> 170 us  [on_device(): pl.pallas_call(kernel, out_shape=(field, field), in_specs=[vmem] * 4 + [s...]
    eq x160 -> x0, other arithmetic: 159 us -> none  [advance(): orders == degree]
    slice x52 -> x0, local copies, waits for them, and re-layouts: 39.7 us -> none  [the longest x32 19.4 us: legendre(): _, table = lax.scan(advance, (zeros, zeros), jnp.arange(LMAX), unroll=8)]
    dot_general x10 -> x0, matrix products: 37 us -> none  [the longest x2 15 us: on_device(): jnp.einsum('lam,lkcm->kacm', table, collect(pot_coeffs, 'lat', 0), precis...]
    all_to_all x2 -> x0, waiting for transfers between devices: 27.4 us -> none  [sum_at_owner(): lax.all_to_all(split_up(array, dim, devices), axis, 0, 0, tiled=True)]
    while x224 -> x0, other arithmetic: 23.8 us -> none
  transfers between devices with their start and end apart: 10 -> 0, of which waited for: 8 -> 0; matrix products, arithmetic and copies ran while one was open for 25% -> 0% of each run, Pallas kernels for 0% -> 0%
where the time goes in v1:
time: 173 us
  Pallas kernels  170 us (98%)
  local copies, waits for them, and re-layouts  2.57 us (1%)
    pallas_call x1, Pallas kernels, on_device(): pl.pallas_call(kernel, out_shape=(field, field), in_specs=[vmem] * 4 + [s...  170 us

profile of v1, /device:TPU:1, one launch (start us, length us, event | category | flops | bytes accessed | tf_op | source)
XLA Modules:
  0.0 172.9 jit_solution(10092316343260101755)
XLA Ops:
  0.6 169.6 %shard_map.95 = (f32[32,24,128]{2,1,0:T(8,128)}, f32[32,24,128]{2,1,0:T(8,128)}) custom-call(f32[32,24,128]{2,1,0:T(8,128)} %u_in.1, s32[32,24,128]{2,1,0:T(8,128)} %mat_in.1, s32[24,128]{1,0:T(8,128)} %mask_in.1, f32[24,128]{1,0:T(8,128)} %ice_in.1, f32[4]{0:T(128)} %shear.1, f32[4]{0:T(128)} %restoring.1, f32[4]{0:T(128)} %contrast.1, f32[16,32,32]{2,1,0:T(8,128)} %green_in.1), custom_call_target="tpu_custom_call" | custom-call | tf_op jit(solution)/shard_map/pallas_call | solution.py:703
  170.3 0.0 copy-start
  170.3 1.8 %copy.12 = f32[32,24,128]{2,1,0:T(8,128)} copy(f32[32,24,128]{2,1,0:T(8,128)} %get-tuple-element.4) | data formatting | bytes 786432
  172.1 0.0 copy-done
  172.1 0.7 copy.13
Async XLA Ops:
  170.3 1.8 %copy-start = (f32[32,24,128]{2,1,0:T(8,128)S(1)}, f32[32,24,128]{2,1,0:T(8,128)}, u32[]{:S(2)}) copy-start(f32[32,24,128]{2,1,0:T(8,128)} %get-tuple-element.5) | copy-start | bytes 1179652

commit v2 on v1

--- a/solution.py
+++ b/solution.py
@@ -37,6 +37,15 @@
 
 def dot_t(a, b):
     return lax.dot_general(a, b, (((1,), (1,)), ((), ())), preferred_element_type=F32)
+
+
+def unrolled(total, factor, one):
+    def body(step, carry):
+        for part in range(factor):
+            one(step * factor + part)
+        return carry
+
+    lax.fori_loop(0, total // factor, body, 0)
 
 
 def lookup(mat, table):
@@ -75,11 +84,12 @@
     T2,
     R2,
     AH,
-    C3,
     T3,
     R3,
     T4,
     R4,
+    RH,
+    RL,
     XH,
     Y,
     T5,
@@ -88,7 +98,7 @@
     T6,
     R6,
     GR,
-    Pf,
+    GX,
     Ph,
     Pl,
     matf,
@@ -153,28 +163,27 @@
         wrow[0:ROWS, :] = w
         wrow[ROWS:, :] = w
         Z[...] = jnp.zeros_like(Z)
-        C3[...] = jnp.zeros_like(C3)
         for b in range(2):
             U[b, 0] = jnp.zeros((32, 256), F32)
             U[b, L + 1] = jnp.zeros((32, 256), F32)
 
     def prepare():
-        def one(k, carry):
+        def one(k):
             mat = mat_in[k]
             matf[k] = mat.astype(F32)
             rho[k] = lookup(mat, contrast)
-            return carry
-
-        lax.fori_loop(0, L, one, 0)
+            U[0, k + 1, 0:ROWS, 0:COLS] = u_in[k]
+
+        unrolled(L, 4, one)
         load[...] = mask_in[...].astype(F32) * ice_in[...]
 
     lane24 = iota((ROWS, COLS), 1)
 
     def pack(read, g):
-        def one(kk, acc):
-            return jnp.where(lane24 // 8 == kk, pltpu.roll(read(16 * g + kk), 8 * kk + 4, 1), acc)
-
-        return lax.fori_loop(0, 16, one, jnp.zeros((ROWS, COLS), F32))
+        acc = jnp.zeros((ROWS, COLS), F32)
+        for kk in range(16):
+            acc = jnp.where(lane24 // 8 == kk, pltpu.roll(read(16 * g + kk), (8 * kk + 4) % COLS, 1), acc)
+        return acc
 
     left = lax.rem(me_lon + N - 1, N)
     right = lax.rem(me_lon + 1, N)
@@ -228,7 +237,7 @@
     inside8 = inside[24:32, 0:COLS]
 
     def pair_u(base):
-        def one(k, carry):
+        def one(k):
             pair_rows(
                 base + k,
                 U[0, k + 1, 0:8, 0:COLS],
@@ -236,9 +245,8 @@
                 U[0, k + 17, 0:8, 0:COLS],
                 U[0, k + 17, 16:24, 0:COLS],
             )
-            return carry
-
-        lax.fori_loop(0, 16, one, 0)
+
+        unrolled(16, 4, one)
         pair_rows(base + 16, PK[0, 0:8], PK[0, 16:24], PK[1, 0:8], PK[1, 16:24])
 
     def fill_u(base):
@@ -246,17 +254,16 @@
         PK[0, 24:32] = jnp.where(inside8, first, 0.0)
         PK[1, 24:32] = jnp.where(inside8, second, 0.0)
 
-        def one(k, carry):
+        def one(k):
             first, second = halo_rows(base + k)
             U[0, k + 1, 24:32, 0:COLS] = jnp.where(inside8, first, 0.0)
             U[0, k + 17, 24:32, 0:COLS] = jnp.where(inside8, second, 0.0)
             U[0, k + 1, :, COLS:] = pltpu.roll(PK[0], 124 - 8 * k, 1)
             U[0, k + 17, :, COLS:] = pltpu.roll(PK[1], 124 - 8 * k, 1)
-            return carry
-
-        lax.fori_loop(0, 16, one, 0)
-
-    def legendre():
+
+        unrolled(16, 4, one)
+
+    def legendre_setup():
         lane = iota((N, 512), 1)
         order = (iota((N, 512), 0) + me_lat * N).astype(F32)
         aa = lane % 32
@@ -297,24 +304,15 @@
                 value = jnp.where(
                     order_i == degree, diagonal, jnp.where(order_i == degree - 1, start, general)
                 )
-                for tile in range(4):
-                    Pf[tile, pl.ds(pl.multiple_of(degree * N, N), N), :] = value[:, tile * COLS : (tile + 1) * COLS]
+                hi, lo = split(value)
+                here = pl.ds(pl.multiple_of(degree * N, N), N)
+                Ph[here, :] = hi
+                Pl[here, :] = lo
                 one, two = value, one
             return one, two
 
         zeros = jnp.zeros((N, 512), F32)
-        lax.fori_loop(0, LMAX // 8, block, (zeros, zeros))
-
-    def legendre_split():
-        def one(m, carry):
-            for tile in range(4):
-                value = Pf[tile, pl.ds(m, LMAX, stride=N), :]
-                hi, lo = split(value)
-                Ph[m, :, tile * COLS : (tile + 1) * COLS] = hi
-                Pl[m, :, tile * COLS : (tile + 1) * COLS] = lo
-            return carry
-
-        lax.fori_loop(0, N, one, 0)
+        return block, (zeros, zeros)
 
     def exchange(phase, axis, src, dst, peer, sender):
         return pltpu.make_async_remote_copy(
@@ -326,68 +324,86 @@
             device_id_type=MESH,
         )
 
-    def slab(ref, index):
-        return ref.at[pl.ds(pl.multiple_of(index * N, N), N)]
-
-    def swap_start(phase, axis, me, src, dst):
+    def slab(ref, index, size):
+        return ref.at[pl.ds(pl.multiple_of(index * size, size), size)]
+
+    def swap_start(phase, axis, me, src, dst, size):
         def one(d, carry):
             peer = lax.rem(me + d, N)
-            exchange(phase, axis, slab(src, peer), slab(dst, me), peer, me).start()
+            exchange(phase, axis, slab(src, peer, size), slab(dst, me, size), peer, me).start()
             return carry
 
         lax.fori_loop(1, N, one, 0)
-        mine = pl.ds(pl.multiple_of(me * N, N), N)
+        mine = pl.ds(pl.multiple_of(me * size, size), size)
         dst[mine, :] = src[mine, :]
 
-    def swap_wait(phase, axis, me, src, dst):
+    def swap_wait(phase, axis, me, src, dst, size):
         def one(d, carry):
             peer = lax.rem(me + d, N)
-            copy = exchange(phase, axis, slab(src, peer), slab(dst, peer), peer, peer)
+            copy = exchange(phase, axis, slab(src, peer, size), slab(dst, peer, size), peer, peer)
             copy.wait_send()
             copy.wait_recv()
             return carry
 
         lax.fori_loop(1, N, one, 0)
 
-    def sweep(src, dst):
-        def one(k, carry):
-            c = U[src, k + 1]
+    lane32 = iota((32, COLS), 1)
+
+    def sweep(src, dst, last):
+        rows = ROWS if last else 32
+
+        def one(k):
+            t0 = U[src, k + 1, :, 0:COLS]
+            t1 = U[src, k + 1, :, COLS:]
+            r0, r1 = pltpu.roll(t0[0:rows], 1, 1), pltpu.roll(t1[0:rows], 1, 1)
+            l0, l1 = pltpu.roll(t0[0:rows], COLS - 1, 1), pltpu.roll(t1[0:rows], COLS - 1, 1)
+            first = lane32[0:rows] == 0
+            final = lane32[0:rows] == COLS - 1
             around = (
-                pltpu.roll(c, 1, 0)
-                + pltpu.roll(c, 31, 0)
-                + pltpu.roll(c, 1, 1)
-                + pltpu.roll(c, 255, 1)
-                + U[src, k]
-                + U[src, k + 2]
+                (jnp.where(first, r1, r0) + jnp.where(final, l1, l0))
+                + (pltpu.roll(t0, 1, 0) + pltpu.roll(t0, 31, 0))[0:rows]
+                + (U[src, k, 0:rows, 0:COLS] + U[src, k + 2, 0:rows, 0:COLS])
             )
-            U[dst, k + 1] = Ac[k] + Bc[k] * around
-            return carry
-
-        lax.fori_loop(0, L, one, 0)
-
-    def coefficients():
+            U[dst, k + 1, 0:rows, 0:COLS] = Ac[k, 0:rows, 0:COLS] + Bc[k, 0:rows, 0:COLS] * around
+            if not last:
+                around = (
+                    (jnp.where(first, r0, r1) + jnp.where(final, l0, l1))
+                    + (pltpu.roll(t1, 1, 0) + pltpu.roll(t1, 31, 0))
+                    + (U[src, k, :, COLS:] + U[src, k + 2, :, COLS:])
+                )
+                U[dst, k + 1, :, COLS:] = Ac[k, :, COLS:] + Bc[k, :, COLS:] * around
+
+        unrolled(L, 4, one)
+
+    def coefficient(k, rows, cols, mat, valid):
+        st = lookup(mat, shear)
+        re = lookup(mat, restoring)
+        inv = 1.0 / (6.0 * st + re)
+        if valid is not None:
+            inv = jnp.where(valid, inv, 0.0)
+        Rd[k, rows, cols] = inv
+        Bc[k, rows, cols] = st * inv
+        Ac[k, rows, cols] = jnp.zeros(inv.shape, F32)
+
+    def main_coefficients():
+        unrolled(L, 4, lambda k: coefficient(k, slice(0, ROWS), slice(0, COLS), matf[k], None))
+
+    inside_side = inside[:, 0:COLS]
+
+    def margin_coefficients():
         first, second = halo_rows(33)
         PK[2, 24:32] = first
         PK[3, 24:32] = second
 
-        def one(k, carry):
-            low = []
+        def one(k):
             first, second = halo_rows(17 + k)
-            for kk, rows in ((k, first), (k + 16, second)):
-                g = 2 if len(low) == 0 else 3
-                low.append(g)
-                main = jnp.concatenate([matf[kk], rows], axis=0)
-                side = pltpu.roll(PK[g], 124 - 8 * k, 1)
-                mat = jnp.concatenate([main, side], axis=1)
-                st = lookup(mat, shear)
-                re = lookup(mat, restoring)
-                inv = jnp.where(inside, 1.0 / (6.0 * st + re), 0.0)
-                Rd[kk] = inv
-                Bc[kk] = st * inv
-                Ac[kk] = jnp.zeros((32, 256), F32)
-            return carry
-
-        lax.fori_loop(0, 16, one, 0)
+            coefficient(k, slice(ROWS, 32), slice(0, COLS), first, inside8)
+            coefficient(k + 16, slice(ROWS, 32), slice(0, COLS), second, inside8)
+            for g in range(2):
+                side = pltpu.roll(PK[2 + g], 124 - 8 * k, 1)
+                coefficient(k + 16 * g, slice(0, 32), slice(COLS, 2 * COLS), side, inside_side)
+
+        unrolled(16, 2, one)
         first, second = halo_rows(34)
         PK[4, 24:32] = second
         loadx[0:ROWS, 0:COLS] = load[...]
@@ -396,32 +412,39 @@
         Ac[0] = loadx[...] * Rd[0]
 
     lane16 = iota((N, COLS), 1)
-    rowmod = iota((64, LMAX), 0) % N
-    rowmod_w = iota((64, 512), 0) % N
+    diagonal64 = iota((64, LMAX), 0) % N == iota((64, LMAX), 1) % N
+    diagonal16 = iota((N, COLS), 0) == iota((N, COLS), 1) % N
 
     def forward_fourier():
-        def part(p, acc):
+        def pair(step, acc):
             acc_c, acc_s = acc
-            x = R1[p].reshape(2 * ROWS, COLS)
-            hi, lo = split(x)
-            r = dot(jnp.concatenate([hi, lo], axis=0), FH[...])
-            r = r[0 : 2 * ROWS] + r[2 * ROWS :] + dot(hi, FL[...])
-            yc = r[:, 0:LMAX]
-            ys = r[:, LMAX:]
-            c = C16[pl.ds(p, 1), :]
-            s = S16[pl.ds(p, 1), :]
-            return acc_c + (c * yc - s * ys), acc_s + (s * yc + c * ys)
-
-        def one(d, acc):
+            ps = [lax.rem(me_lon + 2 * step + q, N) for q in range(2)]
+            his, los = zip(*[split(R1[p].reshape(2 * ROWS, COLS)) for p in ps])
+            r = dot(jnp.concatenate(his + los, axis=0), FH[...])
+            r = r[0 : 4 * ROWS] + r[4 * ROWS :] + dot(jnp.concatenate(his, axis=0), FL[...])
+            for q, p in enumerate(ps):
+                yc = r[2 * ROWS * q : 2 * ROWS * (q + 1), 0:LMAX]
+                ys = r[2 * ROWS * q : 2 * ROWS * (q + 1), LMAX:]
+                c = C16[pl.ds(p, 1), :]
+                s = S16[pl.ds(p, 1), :]
+                acc_c, acc_s = acc_c + (c * yc - s * ys), acc_s + (s * yc + c * ys)
+            return acc_c, acc_s
+
+        def wait(d):
             p = lax.rem(me_lon + d, N)
             copy = exchange(0, "lon", dens.at[p], R1.at[p], p, p)
             copy.wait_send()
             copy.wait_recv()
-            return part(p, acc)
+
+        def one(step, acc):
+            wait(2 * step)
+            wait(2 * step + 1)
+            return pair(step, acc)
 
         zeros = jnp.zeros((2 * ROWS, LMAX), F32)
         R1[me_lon] = dens[me_lon]
-        acc_c, acc_s = lax.fori_loop(1, N, one, part(me_lon, (zeros, zeros)))
+        wait(1)
+        acc_c, acc_s = lax.fori_loop(1, N // 2, one, pair(0, (zeros, zeros)))
         for c, acc in ((0, acc_c), (1, acc_s)):
             acc = acc * wrow[...]
             for kk in range(2):
@@ -441,35 +464,71 @@
                 AH[ck * N : (ck + 1) * N, t * COLS : (t + 1) * COLS] = hi
                 AH[64 + ck * N : 64 + (ck + 1) * N, t * COLS : (t + 1) * COLS] = lo
 
-        def one(m, acc):
-            r = dot_t(AH[...], Ph[m])
-            r = r[0:64] + r[64:] + dot_t(AH[0:64], Pl[m])
-            return jnp.where(rowmod == m, r, acc)
-
-        C3[0:64, :] = lax.fori_loop(0, N, one, jnp.zeros((64, LMAX), F32))
-        T3[...] = jnp.transpose(C3[...])
+        def one(d, carry):
+            b = lax.rem(me_lon + d, N)
+            here = pl.ds(pl.multiple_of(b * LMAX, LMAX), LMAX)
+            r = dot_t(AH[...], Ph[here, :])
+            r = r[0:64] + r[64:] + dot_t(AH[0:64], Pl[here, :])
+            r = jnp.where(diagonal64, r, 0.0)
+            out = []
+            for ck in range(4):
+                half = r[ck * N : ck * N + 8] + r[ck * N + 8 : ck * N + 16]
+                total = jnp.sum(half, axis=0, keepdims=True)
+                out += [total[:, 0:COLS], total[:, COLS:]]
+            T3[pl.ds(pl.multiple_of(b * 8, 8), 8), :] = jnp.concatenate(out, axis=0)
+
+            @pl.when(d < N)
+            def _():
+                exchange(2, "lon", slab(T3, b, 8), slab(R3, me_lon, 8), b, me_lon).start()
+
+            return carry
+
+        lax.fori_loop(1, N + 1, one, 0)
+        mine = pl.ds(pl.multiple_of(me_lon * 8, 8), 8)
+        R3[mine, :] = T3[mine, :]
+
+    def expand_green():
+        chosen = (iota((N, LMAX), 0) == iota((N, LMAX), 1) // N).astype(F32)
+        out = lax.dot_general(
+            GR[...], chosen, (((0,), (0,)), ((), ())), precision=lax.Precision.HIGHEST, preferred_element_type=F32
+        )
+        GX[0] = out[:, 0:COLS]
+        GX[1] = out[:, COLS:]
 
     def layer_sum():
-        even = (lane16 // 16) % 2 == 0
-        for l in range(N):
-            r = R3[pl.ds(l, N, stride=N), :]
-            r = jnp.concatenate([r, pltpu.roll(r, COLS - 16, 1)], axis=0)
-            out = jnp.dot(GR[l], r, precision=lax.Precision.HIGHEST, preferred_element_type=F32)
-            T4[pl.ds(l, N, stride=N), :] = jnp.where(even, out[0:N], pltpu.roll(out[N:], 16, 1))
+        for t in range(2):
+            acc = [jnp.zeros((L, COLS), F32), jnp.zeros((L, COLS), F32)]
+            for k in range(L):
+                kk, j = k // N, k % N
+                g = GX[t, pl.ds(k, L, stride=L), :]
+                for c in range(2):
+                    row = j * 8 + (2 * c + kk) * 2 + t
+                    acc[c] = acc[c] + g * R3[row : row + 1, :]
+            for c in range(2):
+                for kk in range(2):
+                    T4[pl.ds((2 * c + kk) * 2 + t, N, stride=8), :] = acc[c][kk * N : (kk + 1) * N]
 
     def inverse_legendre():
-        hi, lo = split(jnp.transpose(R4[...])[0:64])
-        XH[0:64, :] = hi
-        XH[64:, :] = lo
-
-        def one(m, carry):
-            r = dot(XH[...], Ph[m])
-            r = r[0:64] + r[64:] + dot(XH[0:64], Pl[m])
-            Y[...] = jnp.where(rowmod_w == m, r, Y[...])
-            return carry
-
-        Y[...] = jnp.zeros_like(Y)
-        lax.fori_loop(0, N, one, 0)
+        x = R4[...]
+        hi = x.astype(BF16).astype(F32)
+        RH[...] = hi
+        RL[...] = x - hi
+
+        def one(step, acc):
+            for part in range(4):
+                b = step * 4 + part
+                for ck in range(4):
+                    for t in range(2):
+                        row = pl.ds(b * 8 + ck * 2 + t, 1)
+                        cols = slice(part * LMAX + t * COLS, part * LMAX + (t + 1) * COLS)
+                        for base, ref in ((0, RH), (64, RL)):
+                            v = jnp.where(diagonal16, ref[row, :], 0.0)
+                            XH[base + ck * N : base + (ck + 1) * N, cols] = v.astype(BF16)
+            here = pl.ds(pl.multiple_of(step * 4 * LMAX, LMAX), 4 * LMAX)
+            r = dot(XH[...], Ph[here, :])
+            return acc + (r[0:64] + r[64:] + dot(XH[0:64], Pl[here, :]))
+
+        Y[...] = lax.fori_loop(0, 4, one, jnp.zeros((64, 512), F32))
         for i in range(N):
             t, ii = i // 4, i % 4
             out = None
@@ -482,37 +541,58 @@
 
     lane8 = iota((8, COLS), 1)
 
-    def inverse_fourier():
+    def inverse_fourier(final):
         X5[...] = jnp.transpose(R5[...])
-
-        def one(d, carry):
-            p = lax.rem(me_lon + d, N)
-            c = C16[pl.ds(p, 1), :]
-            s = S16[pl.ds(p, 1), :]
-            a = X5[0:64, :]
-            b = X5[64:, :]
-            x = jnp.concatenate([a * c + b * s, b * c - a * s], axis=1)
-            hi, lo = split(x)
-            r = dot(jnp.concatenate([hi, lo], axis=0), WH[...])
-            r = r[0:64] + r[64:] + dot(hi, WL[...])
-            T6[p, 0:64, :] = r[:, 0:COLS]
-            side = r[0:8, COLS:]
-            for t in range(1, 8):
-                side = jnp.where(lane8 // 8 == t, pltpu.roll(r[8 * t : 8 * t + 8, COLS:], 8 * t, 1), side)
-            T6[p, 64:72, :] = side
-
-            @pl.when(d < N)
-            def _():
-                exchange(5, "lon", T6.at[p], R6.at[me_lon], p, me_lon).start()
+        height = ROWS if final else 32
+        rows = 2 * height
+        size = rows if final else 72
+        width = COLS if final else 2 * COLS
+
+        def own(base):
+            return jnp.concatenate([X5[base + kk * 32 : base + kk * 32 + height, :] for kk in range(2)], axis=0)
+
+        def piece(p):
+            return T6.at[p, pl.ds(0, size)], R6.at[me_lon, pl.ds(0, size)], R6.at[p, pl.ds(0, size)]
+
+        def one(step, carry):
+            ps = [lax.rem(me_lon + 1 + 2 * step + q, N) for q in range(2)]
+            his, los = [], []
+            a, b = own(0), own(64)
+            for p in ps:
+                c = C16[pl.ds(p, 1), :]
+                s = S16[pl.ds(p, 1), :]
+                hi, lo = split(jnp.concatenate([a * c + b * s, b * c - a * s], axis=1))
+                his.append(hi)
+                los.append(lo)
+            r = dot(jnp.concatenate(his + los, axis=0), WH[:, 0:width])
+            both = r[0 : 2 * rows] + r[2 * rows :] + dot(jnp.concatenate(his, axis=0), WL[:, 0:width])
+            for q, p in enumerate(ps):
+                r = both[q * rows : (q + 1) * rows]
+                T6[p, 0:rows, :] = r[:, 0:COLS]
+                if not final:
+                    side = r[0:8, COLS:]
+                    for t in range(1, 8):
+                        v = pltpu.roll(r[8 * t : 8 * t + 8, COLS:], 8 * t, 1)
+                        side = jnp.where(lane8 // 8 == t, v, side)
+                    T6[p, 64:72, :] = side
+                src, dst, _ = piece(p)
+                if q == 0:
+                    exchange(5, "lon", src, dst, p, me_lon).start()
+                else:
+
+                    @pl.when(step < N // 2 - 1)
+                    def _():
+                        exchange(5, "lon", src, dst, p, me_lon).start()
 
             return carry
 
-        lax.fori_loop(1, N + 1, one, 0)
-        R6[me_lon] = T6[me_lon]
+        lax.fori_loop(0, N // 2, one, 0)
+        R6[me_lon, 0:size] = T6[me_lon, 0:size]
 
         def wait(d, carry):
             p = lax.rem(me_lon + d, N)
-            copy = exchange(5, "lon", T6.at[p], R6.at[p], p, p)
+            src, _, dst = piece(p)
+            copy = exchange(5, "lon", src, dst, p, p)
             copy.wait_send()
             copy.wait_recv()
             return carry
@@ -526,7 +606,7 @@
                 dens[q, kk] = rho[k] * U[0, k + 1, 0:ROWS, 0:COLS]
             return carry
 
-        lax.fori_loop(0, N, one, 0)
+        lax.fori_loop(0, N // 2, lambda h, c: one(2 * h + 1, one(2 * h, c)), 0)
 
         def start(d, carry):
             p = lax.rem(me_lon + d, N)
@@ -535,32 +615,29 @@
 
         lax.fori_loop(1, N, start, 0)
 
-    def load_u(k, carry):
-        U[0, k + 1, 0:ROWS, 0:COLS] = u_in[k]
-        return carry
-
     prepare()
-    lax.fori_loop(0, L, load_u, 0)
     E[0] = pack(lambda k: u_in[k], 0)
     E[1] = pack(lambda k: u_in[k], 1)
     E[2] = pack(lambda k: matf[k], 0)
     E[3] = pack(lambda k: matf[k], 1)
     E[4] = pltpu.roll(load[...], 4, 1)
+    tables()
+    block, state = legendre_setup()
+    state = lax.fori_loop(0, 2, block, state)
     pl.semaphore_wait(barrier, 2 * N - 1)
     edges = edge_copies(0)
     for copy in edges:
         copy.start()
-    tables()
+    state = lax.fori_loop(2, 14, block, state)
     for copy in edges:
         copy.wait()
     merge_edges(0)
     pair_u(0)
 
-    def pair_mat(k, carry):
+    def pair_mat(k):
         pair_rows(17 + k, matf[k, 0:8], matf[k, 16:24], matf[k + 16, 0:8], matf[k + 16, 16:24])
-        return carry
-
-    lax.fori_loop(0, 16, pair_mat, 0)
+
+    unrolled(16, 4, pair_mat)
     pair_rows(33, PK[2, 0:8], PK[2, 16:24], PK[3, 0:8], PK[3, 16:24])
     pair_rows(34, load[0:8], load[16:24], PK[4, 0:8], PK[4, 16:24])
     rows = row_copies(0)
@@ -575,12 +652,12 @@
         device_id_type=MESH,
     )
     green.start()
-    legendre()
-    legendre_split()
+    lax.fori_loop(14, 32, block, state)
+    main_coefficients()
     for copy in rows:
         copy.wait()
     fill_u(0)
-    coefficients()
+    margin_coefficients()
 
     for it in range(2):
         if it == 1:
@@ -588,7 +665,7 @@
                 copy.wait()
             fill_u(35)
 
-            def force(j, carry):
+            def force(j):
                 side = R6[j, 64:72, :]
                 for kk in range(2):
                     k = kk * N + j
@@ -597,32 +674,31 @@
                         [pltpu.roll(side, 124 - 8 * (4 * kk + g), 1) for g in range(4)], axis=0
                     )
                     Ac[k] = jnp.concatenate([main, halo], axis=1) * Rd[k]
-                return carry
-
-            lax.fori_loop(0, N, force, 0)
+
+            unrolled(N, 2, force)
             Ac[0] = Ac[0] + loadx[...] * Rd[0]
         for s in range(SWEEPS):
-            sweep(s % 2, (s + 1) % 2)
+            sweep(s % 2, (s + 1) % 2, s == SWEEPS - 1)
         send_density()
         if it == 0:
             E[5] = pack(lambda k: U[0, k + 1, 0:ROWS, 0:COLS], 0)
             E[6] = pack(lambda k: U[0, k + 1, 0:ROWS, 0:COLS], 1)
         else:
 
-            def store_u(k, carry):
+            def store_u(k):
                 u_out[k] = U[0, k + 1, 0:ROWS, 0:COLS]
-                return carry
-
-            lax.fori_loop(0, L, store_u, 0)
+
+            unrolled(L, 4, store_u)
         forward_fourier()
-        swap_start(1, "lat", me_lat, T2, R2)
+        swap_start(1, "lat", me_lat, T2, R2, N)
         if it == 0:
             edges = edge_copies(1)
             for copy in edges:
                 copy.start()
-        swap_wait(1, "lat", me_lat, T2, R2)
+            green.wait()
+            expand_green()
+        swap_wait(1, "lat", me_lat, T2, R2, N)
         forward_legendre()
-        swap_start(2, "lon", me_lon, T3, R3)
         if it == 0:
             for copy in edges:
                 copy.wait()
@@ -631,22 +707,20 @@
             rows = row_copies(1)
             for copy in rows:
                 copy.start()
-            green.wait()
-        swap_wait(2, "lon", me_lon, T3, R3)
+        swap_wait(2, "lon", me_lon, T3, R3, 8)
         layer_sum()
-        swap_start(3, "lon", me_lon, T4, R4)
-        swap_wait(3, "lon", me_lon, T4, R4)
+        swap_start(3, "lon", me_lon, T4, R4, 8)
+        swap_wait(3, "lon", me_lon, T4, R4, 8)
         inverse_legendre()
-        swap_start(4, "lat", me_lat, T5, R5)
-        swap_wait(4, "lat", me_lat, T5, R5)
-        inverse_fourier()
-
-    def store_pot(j, carry):
+        swap_start(4, "lat", me_lat, T5, R5, N)
+        swap_wait(4, "lat", me_lat, T5, R5, N)
+        inverse_fourier(it == 1)
+
+    def store_pot(j):
         for kk in range(2):
-            pot_out[kk * N + j] = R6[j, kk * 32 : kk * 32 + ROWS, :]
-        return carry
-
-    lax.fori_loop(0, N, store_pot, 0)
+            pot_out[kk * N + j] = R6[j, kk * ROWS : (kk + 1) * ROWS, :]
+
+    unrolled(N, 4, store_pot)
 
 
 def on_device(displacement, materials, ice_mask, ice_height, shear, restoring, contrast, green):
@@ -672,22 +746,23 @@
         ((LMAX, COLS), F32),
         ((LMAX, COLS), F32),
         ((128, 512), BF16),
-        ((128, LMAX), F32),
-        ((LMAX, COLS), F32),
-        ((LMAX, COLS), F32),
-        ((LMAX, COLS), F32),
-        ((LMAX, COLS), F32),
-        ((128, LMAX), BF16),
+        ((8 * N, COLS), F32),
+        ((8 * N, COLS), F32),
+        ((8 * N, COLS), F32),
+        ((8 * N, COLS), F32),
+        ((8 * N, COLS), F32),
+        ((8 * N, COLS), F32),
+        ((128, 4 * LMAX), BF16),
         ((64, 512), F32),
         ((LMAX, COLS), F32),
         ((LMAX, COLS), F32),
         ((128, LMAX), F32),
         ((N, 72, COLS), F32),
         ((N, 72, COLS), F32),
-        ((N, L, L), F32),
-        ((4, LMAX * N, COLS), F32),
-        ((N, LMAX, 512), BF16),
-        ((N, LMAX, 512), BF16),
+        ((N, L * L), F32),
+        ((2, L * L, COLS), F32),
+        ((N * LMAX, 512), BF16),
+        ((N * LMAX, 512), BF16),
         ((L, ROWS, COLS), F32),
         ((ROWS, COLS), F32),
         ((32, 256), F32),
@@ -716,7 +791,7 @@
         compiler_params=pltpu.CompilerParams(
             collective_id=0, has_side_effects=True, vmem_limit_bytes=60 * 1024 * 1024
         ),
-    )(displacement, materials, ice_mask, ice_height, shear, restoring, contrast, green)
+    )(displacement, materials, ice_mask, ice_height, shear, restoring, contrast, green.reshape(N, L * L))
 
 
 def solution(mesh):

time: 173 us -> 140 us (0.81)
  Pallas kernels: 170 us -> 135 us
    pallas_call x1, Pallas kernels: 170 us -> 135 us  [on_device(): pl.pallas_call(kernel, out_shape=(field, field), in_specs=[vmem] * 4 + [s...]
where the time goes in v2:
time: 140 us
  Pallas kernels  135 us (96%)
  local copies, waits for them, and re-layouts  4.29 us (3%)
    pallas_call x1, Pallas kernels, on_device(): pl.pallas_call(kernel, out_shape=(field, field), in_specs=[vmem] * 4 + [s...  135 us

profile of v2, /device:TPU:1, one launch (start us, length us, event | category | flops | bytes accessed | tf_op | source)
XLA Modules:
  0.0 139.6 jit_solution(88522516651952027)
XLA Ops:
  0.6 1.7 %reshape.7.green_in = f32[16,1024]{1,0:T(8,128)} reshape(f32[16,32,32]{2,1,0:T(8,128)} %param.15) | data formatting | bytes 131072 | tf_op jit(solution)/shard_map/reshape | solution.py:794
  2.3 134.7 %shard_map.95 = (f32[32,24,128]{2,1,0:T(8,128)}, f32[32,24,128]{2,1,0:T(8,128)}) custom-call(f32[32,24,128]{2,1,0:T(8,128)} %u_in.1, s32[32,24,128]{2,1,0:T(8,128)} %mat_in.1, s32[24,128]{1,0:T(8,128)} %mask_in.1, f32[24,128]{1,0:T(8,128)} %ice_in.1, f32[4]{0:T(128)} %shear.1, f32[4]{0:T(128)} %restoring.1, f32[4]{0:T(128)} %contrast.1, ...), custom_call_target="tpu_custom_call" | custom-call | tf_op jit(solution)/shard_map/pallas_call | solution.py:778
  137.0 0.0 copy-start
  137.0 1.8 %copy.12 = f32[32,24,128]{2,1,0:T(8,128)} copy(f32[32,24,128]{2,1,0:T(8,128)} %get-tuple-element.4) | data formatting | bytes 786432
  138.8 0.0 copy-done
  138.8 0.7 copy.13
Async XLA Ops:
  137.0 1.8 %copy-start = (f32[32,24,128]{2,1,0:T(8,128)S(1)}, f32[32,24,128]{2,1,0:T(8,128)}, u32[]{:S(2)}) copy-start(f32[32,24,128]{2,1,0:T(8,128)} %get-tuple-element.5) | copy-start | bytes 1179652

commit v3 on v2

--- a/solution.py
+++ b/solution.py
@@ -84,6 +84,8 @@
     T2,
     R2,
     AH,
+    Qh,
+    Ql,
     T3,
     R3,
     T4,
@@ -91,12 +93,17 @@
     RH,
     RL,
     XH,
-    Y,
     T5,
     R5,
     X5,
     T6,
     R6,
+    mats,
+    masks,
+    ice,
+    GA,
+    GP,
+    GQ,
     GR,
     GX,
     Ph,
@@ -117,6 +124,8 @@
     hsend,
     hrecv,
     gsem,
+    insem,
+    outsem,
 ):
     me_lat = lax.axis_index("lat")
     me_lon = lax.axis_index("lon")
@@ -132,6 +141,17 @@
     pl.semaphore_signal(
         barrier, inc=1, device_id={"lat": me_lon, "lon": lax.rem(me_lat + 1, N)}, device_id_type=MESH
     )
+
+    main = U.at[0, pl.ds(1, L), pl.ds(0, ROWS), pl.ds(0, COLS)]
+    loads = [
+        pltpu.make_async_copy(mat_in, mats, insem.at[0]),
+        pltpu.make_async_copy(u_in, main, insem.at[1]),
+        pltpu.make_async_copy(mask_in, masks, insem.at[2]),
+        pltpu.make_async_copy(ice_in, ice, insem.at[3]),
+        pltpu.make_async_copy(green_in, GA, insem.at[4]),
+    ]
+    for copy in loads:
+        copy.start()
 
     def tables():
         q = iota((COLS, LMAX), 0)
@@ -169,13 +189,12 @@
 
     def prepare():
         def one(k):
-            mat = mat_in[k]
+            mat = mats[k]
             matf[k] = mat.astype(F32)
             rho[k] = lookup(mat, contrast)
-            U[0, k + 1, 0:ROWS, 0:COLS] = u_in[k]
 
         unrolled(L, 4, one)
-        load[...] = mask_in[...].astype(F32) * ice_in[...]
+        load[...] = masks[...].astype(F32) * ice[...]
 
     lane24 = iota((ROWS, COLS), 1)
 
@@ -202,15 +221,29 @@
             ),
         ]
 
-    def row_copies(it):
-        first, count = (0, 35) if it == 0 else (35, 17)
+    def row_copies(it, corners):
+        if it == 0:
+            first, count = (33, 3) if corners else (0, 33)
+        else:
+            first, count = (36, 17)
         part = pl.ds(first, count)
+        one = 4 if corners else 2
         return [
             pltpu.make_async_remote_copy(
-                VT.at[part], WT.at[part], hsend.at[it, 2], hrecv.at[it, 2], device_id={"lat": up}, device_id_type=MESH
+                VT.at[part],
+                WT.at[part],
+                hsend.at[it, one],
+                hrecv.at[it, one],
+                device_id={"lat": up},
+                device_id_type=MESH,
             ),
             pltpu.make_async_remote_copy(
-                VB.at[part], WB.at[part], hsend.at[it, 3], hrecv.at[it, 3], device_id={"lat": down}, device_id_type=MESH
+                VB.at[part],
+                WB.at[part],
+                hsend.at[it, one + 1],
+                hrecv.at[it, one + 1],
+                device_id={"lat": down},
+                device_id_type=MESH,
             ),
         ]
 
@@ -247,10 +280,12 @@
             )
 
         unrolled(16, 4, one)
-        pair_rows(base + 16, PK[0, 0:8], PK[0, 16:24], PK[1, 0:8], PK[1, 16:24])
-
-    def fill_u(base):
-        first, second = halo_rows(base + 16)
+
+    def pair_packed(t, g):
+        pair_rows(t, PK[g, 0:8], PK[g, 16:24], PK[g + 1, 0:8], PK[g + 1, 16:24])
+
+    def fill_u(base, packed):
+        first, second = halo_rows(packed)
         PK[0, 24:32] = jnp.where(inside8, first, 0.0)
         PK[1, 24:32] = jnp.where(inside8, second, 0.0)
 
@@ -327,9 +362,12 @@
     def slab(ref, index, size):
         return ref.at[pl.ds(pl.multiple_of(index * size, size), size)]
 
+    def far_first(d):
+        return lax.rem(d + 6, N - 1) + 1
+
     def swap_start(phase, axis, me, src, dst, size):
         def one(d, carry):
-            peer = lax.rem(me + d, N)
+            peer = lax.rem(me + far_first(d), N)
             exchange(phase, axis, slab(src, peer, size), slab(dst, me, size), peer, me).start()
             return carry
 
@@ -391,12 +429,12 @@
     inside_side = inside[:, 0:COLS]
 
     def margin_coefficients():
-        first, second = halo_rows(33)
+        first, second = halo_rows(34)
         PK[2, 24:32] = first
         PK[3, 24:32] = second
 
         def one(k):
-            first, second = halo_rows(17 + k)
+            first, second = halo_rows(16 + k)
             coefficient(k, slice(ROWS, 32), slice(0, COLS), first, inside8)
             coefficient(k + 16, slice(ROWS, 32), slice(0, COLS), second, inside8)
             for g in range(2):
@@ -404,10 +442,9 @@
                 coefficient(k + 16 * g, slice(0, 32), slice(COLS, 2 * COLS), side, inside_side)
 
         unrolled(16, 2, one)
-        first, second = halo_rows(34)
-        PK[4, 24:32] = second
+        PK[4, 24:32] = halo_rows(35)[0]
         loadx[0:ROWS, 0:COLS] = load[...]
-        loadx[ROWS:, 0:COLS] = first
+        loadx[ROWS:, 0:COLS] = halo_rows(32)[0]
         loadx[:, COLS:] = pltpu.roll(PK[4], 124, 1)
         Ac[0] = loadx[...] * Rd[0]
 
@@ -451,6 +488,14 @@
                 Z[(2 * c + kk) * 32 : (2 * c + kk) * 32 + ROWS, :] = acc[kk * ROWS : (kk + 1) * ROWS]
         T2[...] = jnp.transpose(Z[...])
 
+    def transpose_legendre():
+        def one(b):
+            here = pl.ds(pl.multiple_of(b * LMAX, LMAX), LMAX)
+            for src, dst in ((Ph, Qh), (Pl, Ql)):
+                dst[b] = jnp.transpose(src[here, :])
+
+        unrolled(N, 1, one)
+
     def forward_legendre():
         for t in range(4):
             parts = [R2[(4 * t + ii) * N : (4 * t + ii + 1) * N, :] for ii in range(4)]
@@ -464,36 +509,47 @@
                 AH[ck * N : (ck + 1) * N, t * COLS : (t + 1) * COLS] = hi
                 AH[64 + ck * N : 64 + (ck + 1) * N, t * COLS : (t + 1) * COLS] = lo
 
-        def one(d, carry):
-            b = lax.rem(me_lon + d, N)
-            here = pl.ds(pl.multiple_of(b * LMAX, LMAX), LMAX)
-            r = dot_t(AH[...], Ph[here, :])
-            r = r[0:64] + r[64:] + dot_t(AH[0:64], Pl[here, :])
-            r = jnp.where(diagonal64, r, 0.0)
-            out = []
-            for ck in range(4):
-                half = r[ck * N : ck * N + 8] + r[ck * N + 8 : ck * N + 16]
-                total = jnp.sum(half, axis=0, keepdims=True)
-                out += [total[:, 0:COLS], total[:, COLS:]]
-            T3[pl.ds(pl.multiple_of(b * 8, 8), 8), :] = jnp.concatenate(out, axis=0)
-
-            @pl.when(d < N)
-            def _():
-                exchange(2, "lon", slab(T3, b, 8), slab(R3, me_lon, 8), b, me_lon).start()
-
+        def product(b):
+            r = dot(AH[...], Qh[b])
+            return r[0:64] + r[64:] + dot(AH[0:64], Ql[b])
+
+        def one(step, carry):
+            bs = [lax.rem(me_lon + 1 + 4 * step + q, N) for q in range(4)]
+            products = [product(b) for b in bs]
+            for q, (b, r) in enumerate(zip(bs, products)):
+                r = jnp.where(diagonal64, r, 0.0)
+                totals = [
+                    jnp.sum(r[ck * N : ck * N + 8] + r[ck * N + 8 : ck * N + 16], axis=0, keepdims=True)
+                    for ck in range(4)
+                ]
+                out = [v[:, t * COLS : (t + 1) * COLS] for t in range(2) for v in totals]
+                T3[pl.ds(pl.multiple_of(b * 8, 8), 8), :] = jnp.concatenate(out, axis=0)
+                copy = exchange(2, "lon", slab(T3, b, 8), slab(R3, me_lon, 8), b, me_lon)
+                if q < 3:
+                    copy.start()
+                else:
+                    pl.when(step < 3)(copy.start)
             return carry
 
-        lax.fori_loop(1, N + 1, one, 0)
+        lax.fori_loop(0, 4, one, 0)
         mine = pl.ds(pl.multiple_of(me_lon * 8, 8), 8)
         R3[mine, :] = T3[mine, :]
 
     def expand_green():
         chosen = (iota((N, LMAX), 0) == iota((N, LMAX), 1) // N).astype(F32)
-        out = lax.dot_general(
-            GR[...], chosen, (((0,), (0,)), ((), ())), precision=lax.Precision.HIGHEST, preferred_element_type=F32
-        )
-        GX[0] = out[:, 0:COLS]
-        GX[1] = out[:, COLS:]
+        for g in range(4):
+            for q in range(4):
+                GR[4 * g + q] = GQ[g, :, q * L : (q + 1) * L]
+        for k in range(L):
+            out = lax.dot_general(
+                GR[:, k, :],
+                chosen,
+                (((0,), (0,)), ((), ())),
+                precision=lax.Precision.HIGHEST,
+                preferred_element_type=F32,
+            )
+            GX[0, k * L : (k + 1) * L, :] = out[:, 0:COLS]
+            GX[1, k * L : (k + 1) * L, :] = out[:, COLS:]
 
     def layer_sum():
         for t in range(2):
@@ -502,11 +558,11 @@
                 kk, j = k // N, k % N
                 g = GX[t, pl.ds(k, L, stride=L), :]
                 for c in range(2):
-                    row = j * 8 + (2 * c + kk) * 2 + t
+                    row = j * 8 + t * 4 + 2 * c + kk
                     acc[c] = acc[c] + g * R3[row : row + 1, :]
             for c in range(2):
                 for kk in range(2):
-                    T4[pl.ds((2 * c + kk) * 2 + t, N, stride=8), :] = acc[c][kk * N : (kk + 1) * N]
+                    T4[pl.ds(t * 4 + 2 * c + kk, N, stride=8), :] = acc[c][kk * N : (kk + 1) * N]
 
     def inverse_legendre():
         x = R4[...]
@@ -514,32 +570,53 @@
         RH[...] = hi
         RL[...] = x - hi
 
-        def one(step, acc):
-            for part in range(4):
-                b = step * 4 + part
+        def build(b):
+            for ck in range(4):
+                for t in range(2):
+                    row = pl.ds(b * 8 + t * 4 + ck, 1)
+                    cols = pl.ds(pl.multiple_of(b * LMAX + t * COLS, COLS), COLS)
+                    for base, ref in ((0, RH), (64, RL)):
+                        v = jnp.where(diagonal16, ref[row, :], 0.0)
+                        XH[base + ck * N : base + (ck + 1) * N, cols] = v.astype(BF16)
+
+        unrolled(N, 2, build)
+
+        def half(chunk):
+            lanes = pl.ds(pl.multiple_of(chunk * 2 * COLS, 2 * COLS), 2 * COLS)
+
+            def one(step, acc):
+                here = pl.ds(pl.multiple_of(step * 4 * LMAX, 4 * LMAX), 4 * LMAX)
+                r = dot(XH[:, here], Ph[here, lanes])
+                return acc + (r[0:64] + r[64:] + dot(XH[0:64, here], Pl[here, lanes]))
+
+            y = lax.fori_loop(0, 4, one, jnp.zeros((64, 2 * COLS), F32))
+            for i8 in range(8):
+                t, ii = i8 // 4, i8 % 4
+                out = None
                 for ck in range(4):
-                    for t in range(2):
-                        row = pl.ds(b * 8 + ck * 2 + t, 1)
-                        cols = slice(part * LMAX + t * COLS, part * LMAX + (t + 1) * COLS)
-                        for base, ref in ((0, RH), (64, RL)):
-                            v = jnp.where(diagonal16, ref[row, :], 0.0)
-                            XH[base + ck * N : base + (ck + 1) * N, cols] = v.astype(BF16)
-            here = pl.ds(pl.multiple_of(step * 4 * LMAX, LMAX), 4 * LMAX)
-            r = dot(XH[...], Ph[here, :])
-            return acc + (r[0:64] + r[64:] + dot(XH[0:64], Pl[here, :]))
-
-        Y[...] = lax.fori_loop(0, 4, one, jnp.zeros((64, 512), F32))
-        for i in range(N):
-            t, ii = i // 4, i % 4
-            out = None
-            for ck in range(4):
-                turn = ((ck - ii) * 32) % COLS
-                v = Y[ck * N : (ck + 1) * N, t * COLS : (t + 1) * COLS]
-                v = v if turn == 0 else pltpu.roll(v, turn, 1)
-                out = v if out is None else jnp.where(lane16 // 32 == ck, v, out)
-            T5[i * N : (i + 1) * N, :] = out
+                    turn = ((ck - ii) * 32) % COLS
+                    v = y[ck * N : (ck + 1) * N, t * COLS : (t + 1) * COLS]
+                    v = v if turn == 0 else pltpu.roll(v, turn, 1)
+                    out = v if out is None else jnp.where(lane16 // 32 == ck, v, out)
+                i = chunk * 8 + i8
+                T5[pl.ds(pl.multiple_of(i * N, N), N), :] = out
+
+                @pl.when(i != me_lat)
+                def _():
+                    exchange(4, "lat", slab(T5, i, N), slab(R5, me_lat, N), i, me_lat).start()
+
+        near = me_lat // 8
+        half(1 - near)
+        half(near)
+        mine = pl.ds(pl.multiple_of(me_lat * N, N), N)
+        R5[mine, :] = T5[mine, :]
 
     lane8 = iota((8, COLS), 1)
+
+    def pot_copy(j, kk):
+        return pltpu.make_async_copy(
+            R6.at[j, pl.ds(kk * ROWS, ROWS)], pot_out.at[kk * N + j], outsem.at[2 * j + kk]
+        )
 
     def inverse_fourier(final):
         X5[...] = jnp.transpose(R5[...])
@@ -555,7 +632,9 @@
             return T6.at[p, pl.ds(0, size)], R6.at[me_lon, pl.ds(0, size)], R6.at[p, pl.ds(0, size)]
 
         def one(step, carry):
-            ps = [lax.rem(me_lon + 1 + 2 * step + q, N) for q in range(2)]
+            first = far_first(2 * step + 1)
+            second = jnp.where(step == N // 2 - 1, 0, far_first(2 * step + 2))
+            ps = [lax.rem(me_lon + first, N), lax.rem(me_lon + second, N)]
             his, los = [], []
             a, b = own(0), own(64)
             for p in ps:
@@ -588,6 +667,9 @@
 
         lax.fori_loop(0, N // 2, one, 0)
         R6[me_lon, 0:size] = T6[me_lon, 0:size]
+        if final:
+            for kk in range(2):
+                pot_copy(me_lon, kk).start()
 
         def wait(d, carry):
             p = lax.rem(me_lon + d, N)
@@ -595,6 +677,9 @@
             copy = exchange(5, "lon", src, dst, p, p)
             copy.wait_send()
             copy.wait_recv()
+            if final:
+                for kk in range(2):
+                    pot_copy(p, kk).start()
             return carry
 
         lax.fori_loop(1, N, wait, 0)
@@ -609,61 +694,68 @@
         lax.fori_loop(0, N // 2, lambda h, c: one(2 * h + 1, one(2 * h, c)), 0)
 
         def start(d, carry):
-            p = lax.rem(me_lon + d, N)
+            p = lax.rem(me_lon + far_first(d), N)
             exchange(0, "lon", dens.at[p], R1.at[me_lon], p, me_lon).start()
             return carry
 
         lax.fori_loop(1, N, start, 0)
 
+    for copy in loads:
+        copy.wait()
     prepare()
-    E[0] = pack(lambda k: u_in[k], 0)
-    E[1] = pack(lambda k: u_in[k], 1)
+    E[0] = pack(lambda k: U[0, k + 1, 0:ROWS, 0:COLS], 0)
+    E[1] = pack(lambda k: U[0, k + 1, 0:ROWS, 0:COLS], 1)
     E[2] = pack(lambda k: matf[k], 0)
     E[3] = pack(lambda k: matf[k], 1)
     E[4] = pltpu.roll(load[...], 4, 1)
+    pair_u(0)
+
+    def pair_mat(k):
+        pair_rows(16 + k, matf[k, 0:8], matf[k, 16:24], matf[k + 16, 0:8], matf[k + 16, 16:24])
+
+    unrolled(16, 4, pair_mat)
+    pair_rows(32, load[0:8], load[16:24], load[0:8], load[16:24])
+    for g in range(4):
+        GP[g] = jnp.concatenate([GA[4 * g + q] for q in range(4)], axis=1)
     tables()
     block, state = legendre_setup()
     state = lax.fori_loop(0, 2, block, state)
     pl.semaphore_wait(barrier, 2 * N - 1)
     edges = edge_copies(0)
-    for copy in edges:
+    rows = row_copies(0, False)
+    for copy in edges + rows:
         copy.start()
-    state = lax.fori_loop(2, 14, block, state)
+    state = lax.fori_loop(2, 12, block, state)
     for copy in edges:
         copy.wait()
     merge_edges(0)
-    pair_u(0)
-
-    def pair_mat(k):
-        pair_rows(17 + k, matf[k, 0:8], matf[k, 16:24], matf[k + 16, 0:8], matf[k + 16, 16:24])
-
-    unrolled(16, 4, pair_mat)
-    pair_rows(33, PK[2, 0:8], PK[2, 16:24], PK[3, 0:8], PK[3, 16:24])
-    pair_rows(34, load[0:8], load[16:24], PK[4, 0:8], PK[4, 16:24])
-    rows = row_copies(0)
-    for copy in rows:
+    pair_packed(33, 0)
+    pair_packed(34, 2)
+    pair_rows(35, PK[4, 0:8], PK[4, 16:24], PK[4, 0:8], PK[4, 16:24])
+    corners = row_copies(0, True)
+    for copy in corners:
         copy.start()
+    lax.fori_loop(12, 32, block, state)
+    main_coefficients()
+    for copy in rows + corners:
+        copy.wait()
     green = pltpu.make_async_remote_copy(
-        green_in,
-        GR,
+        GP,
+        GQ,
         gsem.at[0],
         gsem.at[1],
         device_id={"lat": lax.rem(me_lon + N - 1, N), "lon": me_lat},
         device_id_type=MESH,
     )
     green.start()
-    lax.fori_loop(14, 32, block, state)
-    main_coefficients()
-    for copy in rows:
-        copy.wait()
-    fill_u(0)
+    fill_u(0, 33)
     margin_coefficients()
 
     for it in range(2):
         if it == 1:
             for copy in rows:
                 copy.wait()
-            fill_u(35)
+            fill_u(36, 52)
 
             def force(j):
                 side = R6[j, 64:72, :]
@@ -684,47 +776,46 @@
             E[5] = pack(lambda k: U[0, k + 1, 0:ROWS, 0:COLS], 0)
             E[6] = pack(lambda k: U[0, k + 1, 0:ROWS, 0:COLS], 1)
         else:
-
-            def store_u(k):
-                u_out[k] = U[0, k + 1, 0:ROWS, 0:COLS]
-
-            unrolled(L, 4, store_u)
+            u_copy = pltpu.make_async_copy(main, u_out, outsem.at[2 * N])
+            u_copy.start()
         forward_fourier()
         swap_start(1, "lat", me_lat, T2, R2, N)
         if it == 0:
             edges = edge_copies(1)
             for copy in edges:
                 copy.start()
-            green.wait()
-            expand_green()
+            transpose_legendre()
         swap_wait(1, "lat", me_lat, T2, R2, N)
         forward_legendre()
         if it == 0:
             for copy in edges:
                 copy.wait()
             merge_edges(1)
-            pair_u(35)
-            rows = row_copies(1)
+            pair_u(36)
+            pair_packed(52, 0)
+            rows = row_copies(1, False)
             for copy in rows:
                 copy.start()
+            green.wait()
+            expand_green()
         swap_wait(2, "lon", me_lon, T3, R3, 8)
         layer_sum()
         swap_start(3, "lon", me_lon, T4, R4, 8)
         swap_wait(3, "lon", me_lon, T4, R4, 8)
         inverse_legendre()
-        swap_start(4, "lat", me_lat, T5, R5, N)
         swap_wait(4, "lat", me_lat, T5, R5, N)
         inverse_fourier(it == 1)
 
-    def store_pot(j):
+    def finish(j):
         for kk in range(2):
-            pot_out[kk * N + j] = R6[j, kk * ROWS : (kk + 1) * ROWS, :]
-
-    unrolled(N, 4, store_pot)
+            pot_copy(j, kk).wait()
+
+    unrolled(N, 4, finish)
+    u_copy.wait()
 
 
 def on_device(displacement, materials, ice_mask, ice_height, shear, restoring, contrast, green):
-    vmem = pl.BlockSpec(memory_space=pltpu.VMEM)
+    hbm = pl.BlockSpec(memory_space=pl.ANY)
     smem = pl.BlockSpec(memory_space=pltpu.SMEM)
     field = jax.ShapeDtypeStruct((L, ROWS, COLS), F32)
     scratch = [
@@ -746,20 +837,27 @@
         ((LMAX, COLS), F32),
         ((LMAX, COLS), F32),
         ((128, 512), BF16),
+        ((N, 512, LMAX), BF16),
+        ((N, 512, LMAX), BF16),
         ((8 * N, COLS), F32),
         ((8 * N, COLS), F32),
         ((8 * N, COLS), F32),
         ((8 * N, COLS), F32),
         ((8 * N, COLS), F32),
         ((8 * N, COLS), F32),
-        ((128, 4 * LMAX), BF16),
-        ((64, 512), F32),
+        ((128, N * LMAX), BF16),
         ((LMAX, COLS), F32),
         ((LMAX, COLS), F32),
         ((128, LMAX), F32),
         ((N, 72, COLS), F32),
         ((N, 72, COLS), F32),
-        ((N, L * L), F32),
+        ((L, ROWS, COLS), jnp.int32),
+        ((ROWS, COLS), jnp.int32),
+        ((ROWS, COLS), F32),
+        ((N, L, L), F32),
+        ((4, L, COLS), F32),
+        ((4, L, COLS), F32),
+        ((N, L, L), F32),
         ((2, L * L, COLS), F32),
         ((N * LMAX, 512), BF16),
         ((N * LMAX, 512), BF16),
@@ -770,28 +868,30 @@
         ((7, ROWS, COLS), F32),
         ((7, ROWS, COLS), F32),
         ((5, 32, COLS), F32),
-        ((52, 8, COLS), F32),
-        ((52, 8, COLS), F32),
-        ((52, 8, COLS), F32),
-        ((52, 8, COLS), F32),
+        ((53, 8, COLS), F32),
+        ((53, 8, COLS), F32),
+        ((53, 8, COLS), F32),
+        ((53, 8, COLS), F32),
     ]
     return pl.pallas_call(
         kernel,
         out_shape=(field, field),
-        in_specs=[vmem] * 4 + [smem] * 3 + [vmem],
-        out_specs=(vmem, vmem),
+        in_specs=[hbm] * 4 + [smem] * 3 + [hbm],
+        out_specs=(hbm, hbm),
         scratch_shapes=[pltpu.VMEM(shape, dtype) for shape, dtype in scratch]
         + [
             pltpu.SemaphoreType.DMA((6, N)),
             pltpu.SemaphoreType.DMA((6, N)),
-            pltpu.SemaphoreType.DMA((2, 4)),
-            pltpu.SemaphoreType.DMA((2, 4)),
+            pltpu.SemaphoreType.DMA((2, 6)),
+            pltpu.SemaphoreType.DMA((2, 6)),
             pltpu.SemaphoreType.DMA((2,)),
+            pltpu.SemaphoreType.DMA((5,)),
+            pltpu.SemaphoreType.DMA((2 * N + 1,)),
         ],
         compiler_params=pltpu.CompilerParams(
             collective_id=0, has_side_effects=True, vmem_limit_bytes=60 * 1024 * 1024
         ),
-    )(displacement, materials, ice_mask, ice_height, shear, restoring, contrast, green.reshape(N, L * L))
+    )(displacement, materials, ice_mask, ice_height, shear, restoring, contrast, green)
 
 
 def solution(mesh):

time: 140 us -> 127 us (0.907)
  Pallas kernels: 135 us -> 124 us
  local copies, waits for them, and re-layouts: 4.29 us -> 2.57 us
    pallas_call x1, Pallas kernels: 135 us -> 124 us  [on_device(): pl.pallas_call(kernel, out_shape=(field, field), in_specs=[hbm] * 4 + [sm...]
    reshape x1 -> x0, local copies, waits for them, and re-layouts: 1.72 us -> none  [on_device(): green.reshape(N, L * L)]
where the time goes in v3:
time: 127 us
  Pallas kernels  124 us (98%)
  local copies, waits for them, and re-layouts  2.57 us (2%)
    pallas_call x1, Pallas kernels, on_device(): pl.pallas_call(kernel, out_shape=(field, field), in_specs=[hbm] * 4 + [sm...  124 us
    unnamed x4, local copies, waits for them, and re-layouts  2.57 us

profile of v3, /device:TPU:1, one launch (start us, length us, event | category | flops | bytes accessed | tf_op | source)
XLA Modules:
  0.0 126.8 jit_solution(6008236300055460445)
XLA Ops:
  0.6 123.6 %shard_map.95 = (f32[32,24,128]{2,1,0:T(8,128)}, f32[32,24,128]{2,1,0:T(8,128)}) custom-call(f32[32,24,128]{2,1,0:T(8,128)} %u_in.1, s32[32,24,128]{2,1,0:T(8,128)} %mat_in.1, s32[24,128]{1,0:T(8,128)} %mask_in.1, f32[24,128]{1,0:T(8,128)} %ice_in.1, f32[4]{0:T(128)} %shear.1, f32[4]{0:T(128)} %restoring.1, f32[4]{0:T(128)} %contrast.1, f32[16,32,32]{2,1,0:T(8,128)} %green_in.1), custom_call_target="tpu_custom_call" | custom-call | tf_op jit(solution)/shard_map/pallas_call | solution.py:876
  124.2 0.0 copy-start
  124.2 1.8 %copy.12 = f32[32,24,128]{2,1,0:T(8,128)} copy(f32[32,24,128]{2,1,0:T(8,128)} %get-tuple-element.4) | data formatting | bytes 786432
  126.0 0.0 copy-done
  126.0 0.7 copy.13
Async XLA Ops:
  124.2 1.8 %copy-start = (f32[32,24,128]{2,1,0:T(8,128)S(1)}, f32[32,24,128]{2,1,0:T(8,128)}, u32[]{:S(2)}) copy-start(f32[32,24,128]{2,1,0:T(8,128)} %get-tuple-element.5) | copy-start | bytes 1179652

commit v4 on v3

--- a/solution.py
+++ b/solution.py
@@ -350,10 +350,14 @@
         return block, (zeros, zeros)
 
     def exchange(phase, axis, src, dst, peer, sender):
+        if 1 <= phase <= 4:
+            sender, slot = 0, 0
+        else:
+            slot = peer
         return pltpu.make_async_remote_copy(
             src,
             dst,
-            send_sem.at[phase, peer],
+            send_sem.at[phase, slot],
             recv_sem.at[phase, sender],
             device_id={axis: peer},
             device_id_type=MESH,
@@ -376,14 +380,10 @@
         dst[mine, :] = src[mine, :]
 
     def swap_wait(phase, axis, me, src, dst, size):
-        def one(d, carry):
-            peer = lax.rem(me + d, N)
-            copy = exchange(phase, axis, slab(src, peer, size), slab(dst, peer, size), peer, peer)
-            copy.wait_send()
-            copy.wait_recv()
-            return carry
-
-        lax.fori_loop(1, N, one, 0)
+        part = pl.ds(0, (N - 1) * size)
+        copy = exchange(phase, axis, src.at[part], dst.at[part], lax.rem(me + 1, N), 0)
+        copy.wait_recv()
+        copy.wait_send()
 
     lane32 = iota((32, COLS), 1)
 
@@ -548,15 +548,15 @@
                 precision=lax.Precision.HIGHEST,
                 preferred_element_type=F32,
             )
-            GX[0, k * L : (k + 1) * L, :] = out[:, 0:COLS]
-            GX[1, k * L : (k + 1) * L, :] = out[:, COLS:]
+            GX[0, pl.ds(k, L, stride=L), :] = out[:, 0:COLS]
+            GX[1, pl.ds(k, L, stride=L), :] = out[:, COLS:]
 
     def layer_sum():
         for t in range(2):
             acc = [jnp.zeros((L, COLS), F32), jnp.zeros((L, COLS), F32)]
             for k in range(L):
                 kk, j = k // N, k % N
-                g = GX[t, pl.ds(k, L, stride=L), :]
+                g = GX[t, k * L : (k + 1) * L, :]
                 for c in range(2):
                     row = j * 8 + t * 4 + 2 * c + kk
                     acc[c] = acc[c] + g * R3[row : row + 1, :]
@@ -612,6 +612,14 @@
         R5[mine, :] = T5[mine, :]
 
     lane8 = iota((8, COLS), 1)
+
+    def force(j):
+        side = R6[j, 64:72, :]
+        for kk in range(2):
+            k = kk * N + j
+            main = R6[j, kk * 32 : (kk + 1) * 32, :]
+            halo = jnp.concatenate([pltpu.roll(side, 124 - 8 * (4 * kk + g), 1) for g in range(4)], axis=0)
+            Ac[k] = jnp.concatenate([main, halo], axis=1) * Rd[k]
 
     def pot_copy(j, kk):
         return pltpu.make_async_copy(
@@ -670,6 +678,8 @@
         if final:
             for kk in range(2):
                 pot_copy(me_lon, kk).start()
+        else:
+            force(me_lon)
 
         def wait(d, carry):
             p = lax.rem(me_lon + d, N)
@@ -680,9 +690,13 @@
             if final:
                 for kk in range(2):
                     pot_copy(p, kk).start()
+            else:
+                force(p)
             return carry
 
         lax.fori_loop(1, N, wait, 0)
+        if not final:
+            Ac[0] = Ac[0] + loadx[...] * Rd[0]
 
     def send_density():
         def one(q, carry):
@@ -752,23 +766,6 @@
     margin_coefficients()
 
     for it in range(2):
-        if it == 1:
-            for copy in rows:
-                copy.wait()
-            fill_u(36, 52)
-
-            def force(j):
-                side = R6[j, 64:72, :]
-                for kk in range(2):
-                    k = kk * N + j
-                    main = R6[j, kk * 32 : (kk + 1) * 32, :]
-                    halo = jnp.concatenate(
-                        [pltpu.roll(side, 124 - 8 * (4 * kk + g), 1) for g in range(4)], axis=0
-                    )
-                    Ac[k] = jnp.concatenate([main, halo], axis=1) * Rd[k]
-
-            unrolled(N, 2, force)
-            Ac[0] = Ac[0] + loadx[...] * Rd[0]
         for s in range(SWEEPS):
             sweep(s % 2, (s + 1) % 2, s == SWEEPS - 1)
         send_density()
@@ -803,6 +800,10 @@
         swap_start(3, "lon", me_lon, T4, R4, 8)
         swap_wait(3, "lon", me_lon, T4, R4, 8)
         inverse_legendre()
+        if it == 0:
+            for copy in rows:
+                copy.wait()
+            fill_u(36, 52)
         swap_wait(4, "lat", me_lat, T5, R5, N)
         inverse_fourier(it == 1)
 

time: 127 us -> 125 us (0.984)
  Pallas kernels: 124 us -> 121 us
    pallas_call x1, Pallas kernels: 124 us -> 121 us  [on_device(): pl.pallas_call(kernel, out_shape=(field, field), in_specs=[hbm] * 4 + [sm...]
where the time goes in v4:
time: 125 us; the launch traced here: 124 us
  Pallas kernels  121 us (97%)
  local copies, waits for them, and re-layouts  2.57 us (2%)
    pallas_call x1, Pallas kernels, on_device(): pl.pallas_call(kernel, out_shape=(field, field), in_specs=[hbm] * 4 + [sm...  121 us
    unnamed x4, local copies, waits for them, and re-layouts  2.57 us

profile of v4, /device:TPU:1, one launch (start us, length us, event | category | flops | bytes accessed | tf_op | source)
XLA Modules:
  0.0 124.5 jit_solution(17351595823313947196)
XLA Ops:
  0.6 121.3 %shard_map.95 = (f32[32,24,128]{2,1,0:T(8,128)}, f32[32,24,128]{2,1,0:T(8,128)}) custom-call(f32[32,24,128]{2,1,0:T(8,128)} %u_in.1, s32[32,24,128]{2,1,0:T(8,128)} %mat_in.1, s32[24,128]{1,0:T(8,128)} %mask_in.1, f32[24,128]{1,0:T(8,128)} %ice_in.1, f32[4]{0:T(128)} %shear.1, f32[4]{0:T(128)} %restoring.1, f32[4]{0:T(128)} %contrast.1, f32[16,32,32]{2,1,0:T(8,128)} %green_in.1), custom_call_target="tpu_custom_call" | custom-call | tf_op jit(solution)/shard_map/pallas_call | solution.py:877
  121.9 0.0 copy-start
  121.9 1.8 %copy.12 = f32[32,24,128]{2,1,0:T(8,128)} copy(f32[32,24,128]{2,1,0:T(8,128)} %get-tuple-element.4) | data formatting | bytes 786432
  123.7 0.0 copy-done
  123.8 0.7 copy.13
Async XLA Ops:
  121.9 1.8 %copy-start = (f32[32,24,128]{2,1,0:T(8,128)S(1)}, f32[32,24,128]{2,1,0:T(8,128)}, u32[]{:S(2)}) copy-start(f32[32,24,128]{2,1,0:T(8,128)} %get-tuple-element.5) | copy-start | bytes 1179652

commit v5 on v4

--- a/solution.py
+++ b/solution.py
@@ -369,6 +369,9 @@
     def far_first(d):
         return lax.rem(d + 6, N - 1) + 1
 
+    def arrival(d):
+        return lax.rem(me_lon + N - far_first(d), N)
+
     def swap_start(phase, axis, me, src, dst, size):
         def one(d, carry):
             peer = lax.rem(me + far_first(d), N)
@@ -455,7 +458,7 @@
     def forward_fourier():
         def pair(step, acc):
             acc_c, acc_s = acc
-            ps = [lax.rem(me_lon + 2 * step + q, N) for q in range(2)]
+            ps = [jnp.where(step == 0, me_lon, arrival(2 * step)), arrival(2 * step + 1)]
             his, los = zip(*[split(R1[p].reshape(2 * ROWS, COLS)) for p in ps])
             r = dot(jnp.concatenate(his + los, axis=0), FH[...])
             r = r[0 : 4 * ROWS] + r[4 * ROWS :] + dot(jnp.concatenate(his, axis=0), FL[...])
@@ -468,7 +471,7 @@
             return acc_c, acc_s
 
         def wait(d):
-            p = lax.rem(me_lon + d, N)
+            p = arrival(d)
             copy = exchange(0, "lon", dens.at[p], R1.at[p], p, p)
             copy.wait_send()
             copy.wait_recv()
@@ -682,7 +685,7 @@
             force(me_lon)
 
         def wait(d, carry):
-            p = lax.rem(me_lon + d, N)
+            p = arrival(d)
             src, _, dst = piece(p)
             copy = exchange(5, "lon", src, dst, p, p)
             copy.wait_send()

time: 125 us -> 124 us (level)
  no operation moved by 1% of the time
where the time goes in v5:
time: 124 us; the launch traced here: 123 us
  Pallas kernels  120 us (97%)
  local copies, waits for them, and re-layouts  2.57 us (2%)
    pallas_call x1, Pallas kernels, on_device(): pl.pallas_call(kernel, out_shape=(field, field), in_specs=[hbm] * 4 + [sm...  120 us
    unnamed x4, local copies, waits for them, and re-layouts  2.57 us

profile of v5, /device:TPU:1, one launch (start us, length us, event | category | flops | bytes accessed | tf_op | source)
XLA Modules:
  0.0 123.5 jit_solution(15933579724827625456)
XLA Ops:
  0.6 120.3 %shard_map.95 = (f32[32,24,128]{2,1,0:T(8,128)}, f32[32,24,128]{2,1,0:T(8,128)}) custom-call(f32[32,24,128]{2,1,0:T(8,128)} %u_in.1, s32[32,24,128]{2,1,0:T(8,128)} %mat_in.1, s32[24,128]{1,0:T(8,128)} %mask_in.1, f32[24,128]{1,0:T(8,128)} %ice_in.1, f32[4]{0:T(128)} %shear.1, f32[4]{0:T(128)} %restoring.1, f32[4]{0:T(128)} %contrast.1, f32[16,32,32]{2,1,0:T(8,128)} %green_in.1), custom_call_target="tpu_custom_call" | custom-call | tf_op jit(solution)/shard_map/pallas_call | solution.py:880
  120.9 0.0 copy-start
  120.9 1.8 %copy.12 = f32[32,24,128]{2,1,0:T(8,128)} copy(f32[32,24,128]{2,1,0:T(8,128)} %get-tuple-element.4) | data formatting | bytes 786432
  122.8 0.0 copy-done
  122.8 0.7 copy.13
Async XLA Ops:
  120.9 1.8 %copy-start = (f32[32,24,128]{2,1,0:T(8,128)S(1)}, f32[32,24,128]{2,1,0:T(8,128)}, u32[]{:S(2)}) copy-start(f32[32,24,128]{2,1,0:T(8,128)} %get-tuple-element.5) | copy-start | bytes 1179652

commit v6 on v5

--- a/solution.py
+++ b/solution.py
@@ -373,12 +373,9 @@
         return lax.rem(me_lon + N - far_first(d), N)
 
     def swap_start(phase, axis, me, src, dst, size):
-        def one(d, carry):
-            peer = lax.rem(me + far_first(d), N)
+        for d in range(1, N):
+            peer = lax.rem(me + (d + 6) % (N - 1) + 1, N)
             exchange(phase, axis, slab(src, peer, size), slab(dst, me, size), peer, me).start()
-            return carry
-
-        lax.fori_loop(1, N, one, 0)
         mine = pl.ds(pl.multiple_of(me * size, size), size)
         dst[mine, :] = src[mine, :]
 
@@ -710,12 +707,9 @@
 
         lax.fori_loop(0, N // 2, lambda h, c: one(2 * h + 1, one(2 * h, c)), 0)
 
-        def start(d, carry):
-            p = lax.rem(me_lon + far_first(d), N)
+        for d in range(1, N):
+            p = lax.rem(me_lon + (d + 6) % (N - 1) + 1, N)
             exchange(0, "lon", dens.at[p], R1.at[me_lon], p, me_lon).start()
-            return carry
-
-        lax.fori_loop(1, N, start, 0)
 
     for copy in loads:
         copy.wait()

time: 124 us -> 123 us (level)
  no operation moved by 1% of the time
where the time goes in v6:
time: 123 us
  Pallas kernels  120 us (98%)
  local copies, waits for them, and re-layouts  2.57 us (2%)
    pallas_call x1, Pallas kernels, on_device(): pl.pallas_call(kernel, out_shape=(field, field), in_specs=[hbm] * 4 + [sm...  120 us
    unnamed x4, local copies, waits for them, and re-layouts  2.57 us

profile of v6, /device:TPU:1, one launch (start us, length us, event | category | flops | bytes accessed | tf_op | source)
XLA Modules:
  0.0 123.2 jit_solution(13437212469577620681)
XLA Ops:
  0.6 120.0 %shard_map.95 = (f32[32,24,128]{2,1,0:T(8,128)}, f32[32,24,128]{2,1,0:T(8,128)}) custom-call(f32[32,24,128]{2,1,0:T(8,128)} %u_in.1, s32[32,24,128]{2,1,0:T(8,128)} %mat_in.1, s32[24,128]{1,0:T(8,128)} %mask_in.1, f32[24,128]{1,0:T(8,128)} %ice_in.1, f32[4]{0:T(128)} %shear.1, f32[4]{0:T(128)} %restoring.1, f32[4]{0:T(128)} %contrast.1, f32[16,32,32]{2,1,0:T(8,128)} %green_in.1), custom_call_target="tpu_custom_call" | custom-call | tf_op jit(solution)/shard_map/pallas_call | solution.py:874
  120.6 0.0 copy-start
  120.6 1.8 %copy.12 = f32[32,24,128]{2,1,0:T(8,128)} copy(f32[32,24,128]{2,1,0:T(8,128)} %get-tuple-element.4) | data formatting | bytes 786432
  122.5 0.0 copy-done
  122.5 0.7 copy.13
Async XLA Ops:
  120.6 1.8 %copy-start = (f32[32,24,128]{2,1,0:T(8,128)S(1)}, f32[32,24,128]{2,1,0:T(8,128)}, u32[]{:S(2)}) copy-start(f32[32,24,128]{2,1,0:T(8,128)} %get-tuple-element.5) | copy-start | bytes 1179652
